TPU v7x, 32 devices: a whole 2x2x4 slice. The times are simulated.
32 devices in a mesh: ma: 8 (over z, y), row: 4 (over x, core).
Axes of the slice: x: 2, y: 2, z: 4, core: 2. Of those that a mesh axis runs over, the one named last changes fastest.
Arguments:
- velocity: bfloat16 [3, 2, 16, 32, 65], P(None, None, 'row', 'ma'), may hold values from -6 to 6
- vorticity: bfloat16 [3, 2, 16, 32, 65], P(None, None, 'row', 'ma'), may hold values from -6 to 6
- legendre: bfloat16 [32, 65, 384], P('ma'), may hold values from -0.75 to 0.75
- pair_order: int32 [32], P('ma'), may hold values from 0 to 31, each once
- lat_weight: float32 [384], replicated, may hold values from 0.5 to 2
- diffusivity: float32 [16], replicated, may hold values from 0.25 to 2.5
Outputs:
- new_velocity: float32 [3, 2, 16, 32, 65], P(None, None, 'row', 'ma')
Inputs may be any that keep to these rules, and one draw needn't show every extreme that they name: pair_order holds each of 0 to 31 exactly once.
All inputs are finite; a program needn't handle non-finite values.
Results may differ from a plain program's by a relative error of at most 0.0095.
Values may be sent and summed in bfloat16 or wider, within the bound.
A program may use at most 128 MiB of HBM per device.

v0:
```python
import math

import jax
import jax.numpy as jnp
from jax import lax
from jax.sharding import PartitionSpec as P

NLON = 2048


STEP_SIZE = 1.0


def with_halo(cells, sides, width):
    for axis, dim in sides:
        count = lax.axis_size(axis)
        ends = count - 1
        head = lax.slice_in_dim(cells, 0, width, axis=dim)
        tail = lax.slice_in_dim(cells, cells.shape[dim] - width, cells.shape[dim], axis=dim)
        cells = jnp.concatenate(
            [
                lax.ppermute(tail, axis, [(i, (i + 1) % count) for i in range(ends)]),
                cells,
                lax.ppermute(head, axis, [((i + 1) % count, i) for i in range(ends)]),
            ],
            axis=dim,
        )
    return cells


def row_masks(low_order, pack_rows):
    orders_all = pack_rows - 1
    row_index = jnp.arange(pack_rows, dtype=jnp.int32)[None, :]
    low_column = low_order[:, None]
    is_lower = row_index < orders_all - low_column
    not_lower = jnp.logical_not(is_lower)
    even_low = row_index % 2 == 0
    even_high = (row_index + low_column) % 2 == 0
    low_pair = jnp.stack([is_lower & even_low, is_lower & jnp.logical_not(even_low)])
    high_pair = jnp.stack([not_lower & even_high, not_lower & jnp.logical_not(even_high)])
    return jnp.stack([low_pair, high_pair])


def cross_product(velocity_grid, vorticity_grid):
    return jnp.stack(
        [
            velocity_grid[1] * vorticity_grid[2] - velocity_grid[2] * vorticity_grid[1],
            velocity_grid[2] * vorticity_grid[0] - velocity_grid[0] * vorticity_grid[2],
            velocity_grid[0] * vorticity_grid[1] - velocity_grid[1] * vorticity_grid[0],
        ]
    )


def lon_table(column_order, is_imag, lon_start, lon_count):
    lon_index = lon_start + jnp.arange(lon_count, dtype=jnp.int32)
    angle_index = column_order[:, None] * lon_index[None, :] % NLON
    angle_value = angle_index.astype(jnp.float32) * (2.0 * math.pi / NLON)
    return jnp.where(is_imag[:, None], -jnp.sin(angle_value), jnp.cos(angle_value))


def local(velocity, vorticity, legendre, pair_order, lat_weight, diffusivity):
    pair_count = pair_order.shape[0]
    pack_rows = legendre.shape[1]
    half_lat = legendre.shape[2]
    nlat_all = 2 * half_lat
    levels_dev = velocity.shape[2]
    orders_all = pack_rows - 1
    inv_orders = 1.0 / math.sqrt(orders_all)
    inv_lon = 1.0 / math.sqrt(NLON)
    lon_width = NLON // 4
    mask_bool = row_masks(pair_order, pack_rows)
    fields = jnp.concatenate([velocity, vorticity], axis=0)
    masked = fields[None, None] * mask_bool.astype(jnp.bfloat16)[:, :, None, None, None]
    halves = jnp.einsum(
        "oqfilsr,srj->qfliosj", masked, legendre, preferred_element_type=jnp.float32
    )
    north_part = halves[0] + halves[1]
    south_part = halves[0] - halves[1]
    both_parts = jnp.concatenate([north_part, south_part], axis=-1)
    spectral = jnp.transpose(both_parts, (0, 1, 5, 2, 3, 4))
    spectral = spectral.reshape(6, levels_dev, nlat_all, 4 * pair_count).astype(jnp.bfloat16)
    gathered_ids = lax.all_gather(pair_order, "ma", axis=0, tiled=True)
    pair_slots = gathered_ids.reshape(-1, 1, 1, pair_count)
    both_orders = jnp.concatenate([pair_slots, orders_all - 1 - pair_slots], axis=2)
    full_shape = (both_orders.shape[0], 2, 2, pair_count)
    column_order = jnp.broadcast_to(both_orders, full_shape).reshape(-1)
    part_index = jnp.arange(2, dtype=jnp.int32)[None, :, None, None]
    is_imag = jnp.broadcast_to(part_index, full_shape).reshape(-1) == 1
    tables = [
        lon_table(column_order, is_imag, lon_block * lon_width, lon_width).astype(jnp.bfloat16)
        for lon_block in range(4)
    ]
    spec_block = lax.all_to_all(spectral, "ma", split_axis=2, concat_axis=3, tiled=True)
    accumulated = jnp.zeros((3,) + spec_block.shape[1:], jnp.float32)
    for lon_block in range(4):
        table_block = tables[lon_block]
        grid_values = (
            jnp.einsum("flac,cb->flab", spec_block, table_block, preferred_element_type=jnp.float32)
            * inv_orders
        )
        lamb_vector = cross_product(grid_values[:3], grid_values[3:])
        accumulated = accumulated + jnp.einsum(
            "flab,cb->flac",
            lamb_vector,
            table_block.astype(jnp.float32),
            precision=lax.Precision.HIGH,
            preferred_element_type=jnp.float32,
        )
    lamb_spec = (accumulated * inv_lon).astype(jnp.bfloat16)
    selector = jnp.transpose(mask_bool.astype(jnp.float32), (1, 0, 2, 3))[:, None, None, None]
    lamb_block = lax.all_to_all(lamb_spec, "ma", split_axis=3, concat_axis=2, tiled=True)
    item_count = lamb_block.shape[0]
    shaped = lamb_block.astype(jnp.float32).reshape(
        item_count, levels_dev, nlat_all, 2, 2, pair_count
    )
    shaped = jnp.transpose(shaped, (0, 1, 3, 4, 5, 2))
    north_side = shaped[..., :half_lat]
    south_side = shaped[..., half_lat:]
    weighted = jnp.stack(
        [lat_weight * (north_side + south_side), lat_weight * (north_side - south_side)]
    )
    weighted = weighted.astype(jnp.bfloat16)
    projected = jnp.einsum(
        "qfliosj,srj->qfliosr", weighted, legendre, preferred_element_type=jnp.float32
    )
    picked = jnp.sum(projected * selector, axis=(0, 4))
    tendency = jnp.transpose(picked, (0, 2, 1, 3, 4))
    source = velocity.astype(jnp.float32) + STEP_SIZE * tendency
    row_start = lax.axis_index("row") * levels_dev
    level_total = levels_dev * lax.axis_size("row")
    extended = with_halo(source.astype(jnp.bfloat16), (("row", 2),), 2).astype(source.dtype)
    padded_coupling = jnp.pad(diffusivity, (2, 2))
    wide_coupling = lax.dynamic_slice_in_dim(padded_coupling, row_start, levels_dev + 4)[
        None, None, :, None, None
    ]
    inner_coupling = wide_coupling[:, :, 1:-1]
    first_wide = (
        extended[:, :, 1:-1] + inner_coupling * (extended[:, :, :-2] + extended[:, :, 2:])
    ) / (1.0 + 2.0 * inner_coupling)
    global_level = row_start - 1 + jnp.arange(levels_dev + 2, dtype=jnp.int32)
    inside = ((global_level >= 0) & (global_level < level_total)).astype(jnp.float32)
    first_wide = first_wide * inside[None, None, :, None, None]
    own_coupling = wide_coupling[:, :, 2:-2]
    return (source + own_coupling * (first_wide[:, :, :-2] + first_wide[:, :, 2:])) / (
        1.0 + 2.0 * own_coupling
    )


def solution(mesh):
    in_specs = (
        P(None, None, "row", "ma", None),
        P(None, None, "row", "ma", None),
        P("ma", None, None),
        P("ma"),
        P(),
        P(),
    )
    out_specs = P(None, None, "row", "ma", None)
    return jax.shard_map(local, mesh=mesh, in_specs=in_specs, out_specs=out_specs, check_vma=False)
```

profile of v0, /device:TPU:1, one launch (start us, length us, event | category | flops | bytes accessed | tf_op | source)
XLA Modules:
  0.0 95.0 jit_solution(11931700865630016753)
XLA Ops:
  0.0 0.7 broadcast_subtract_fusion.1
  0.7 0.7 fusion.112
  1.5 0.8 pad_maximum_fusion
  3.3 5.8 %copy.72 = bf16[6,4,768,16]{3,1,0,2:T(4,128)(2,1)} copy(bf16[6,4,768,16]{2,1,3,0:T(4,128)(2,1)S(1)} %bitcast.115) | data formatting | bytes 1179648 | tf_op jit(solution)/shard_map/convert_element_type | solution.py:81
  9.1 7.0 %reshape.343 = bf16[8,2,18432]{2,1,0:T(2,128)(2,1)} reshape(bf16[768,6,4,16]{3,2,1,0:T(4,128)(2,1)} %bitcast.112) | data formatting | bytes 1179648
  16.1 6.4 %all-to-all-start = ((bf16[8,2,18432]{2,1,0:T(2,128)(2,1)}), bf16[8,2,18432]{2,1,0:T(2,128)(2,1)S(1)}, u32[]{:S(2)}, u32[]{:S(2)}) async-start(bf16[8,2,18432]{2,1,0:T(2,128)(2,1)} %reshape.343), calls=%async_computation | async-start | bytes 1179648 | tf_op jit(solution)/shard_map/all_to_all | solution.py:93
  23.9 13.4 %all-reduce.1 = s32[32]{0:T(128)S(1)} all-reduce(s32[32]{0:T(128)S(1)} %dynamic-update-slice), channel_id=1, replica_groups=mesh['ma'=8,'row'=4] {'ma'}, use_global_device_ids=true, to_apply=%add.1 | all-reduce | flops 32 | bytes 256
  37.8 4.4 %reshape.344 = bf16[768,6,4,16]{3,2,1,0:T(4,128)(2,1)} reshape(bf16[8,2,18432]{2,1,0:T(2,128)(2,1)S(1)} %all-to-all-done) | data formatting | bytes 1179648
  42.2 6.0 %copy.102 = bf16[6,4,8,96,16]{3,4,2,1,0:T(8,128)(2,1)S(1)} copy(bf16[6,4,8,96,16]{4,1,0,3,2:T(4,128)(2,1)} %bitcast.113) | data formatting | bytes 1179648 | tf_op jit(solution)/shard_map/all_to_all | solution.py:93
  48.2 1.9 %broadcast_multiply_fusion.3 = f32[6,4,96,512]{3,2,1,0:T(8,128)S(1)} fusion(bf16[6,4,96,128]{2,3,1,0:T(8,128)(2,1)S(1)} %bitcast.108, s32[128]{0:T(128)S(1)} %mul.250, pred[128]{0:T(512)(128)(4,1)S(1)} %eq.67), kind=kOutput, calls=%fused_computation.27 | convolution fusion | flops 304283648 | bytes 5309056 | tf_op jit(solution)/shard_map/flac,cb->flab/dot_general | solution.py:98
  50.7 1.9 %broadcast_multiply_fusion.2 = f32[6,4,96,512]{3,2,1,0:T(8,128)S(1)} fusion(bf16[6,4,96,128]{2,3,1,0:T(8,128)(2,1)S(1)} %bitcast.109, s32[512]{0:T(512)S(1)} %iota_add_fusion.2, s32[128]{0:T(128)S(1)} %mul.250, pred[128]{0:T(512)(128)(4,1)S(1)} %eq.67), kind=kOutput, calls=%fused_computation.26 | convolution fusion | flops 304283648 | bytes 5311104 | tf_op jit(solution)/shard_map/flac,cb->flab/dot_general | solution.py:98
  53.1 1.9 %broadcast_multiply_fusion.1 = f32[6,4,96,512]{3,2,1,0:T(8,128)S(1)} fusion(bf16[6,4,96,128]{2,3,1,0:T(8,128)(2,1)S(1)} %bitcast.110, s32[512]{0:T(512)S(1)} %iota_add_fusion.1, s32[128]{0:T(128)S(1)} %mul.250, pred[128]{0:T(512)(128)(4,1)S(1)} %eq.67), kind=kOutput, calls=%fused_computation.25 | convolution fusion | flops 304283648 | bytes 5311104 | tf_op jit(solution)/shard_map/flac,cb->flab/dot_general | solution.py:98
  55.5 1.9 %broadcast_multiply_fusion = f32[6,4,96,512]{3,2,1,0:T(8,128)S(1)} fusion(bf16[6,4,96,128]{2,3,1,0:T(8,128)(2,1)S(1)} %bitcast.111, s32[512]{0:T(512)S(1)} %iota_add_fusion, s32[128]{0:T(128)S(1)} %mul.250, pred[128]{0:T(512)(128)(4,1)S(1)} %eq.67), kind=kOutput, calls=%fused_computation.24 | convolution fusion | flops 304283648 | bytes 5311104 | tf_op jit(solution)/shard_map/flac,cb->flab/dot_general | solution.py:98
  58.0 1.8 %fusion = f32[3,4,96,128]{3,2,1,0:T(8,128)S(1)} fusion(f32[1,4,96,512]{3,2,1,0:T(8,128)S(1)} %get-tuple-element.16, f32[1,4,96,512]{3,2,1,0:T(8,128)S(1)} %get-tuple-element.15, f32[1,4,96,512]{3,2,1,0:T(8,128)S(1)} %get-tuple-element.14, s32[128]{0:T(128)S(1)} %mul.250, pred[128]{0:T(512)(128)(4,1)S(1)} %eq.67), kind=kOutput, calls=%fused_computation | convolution fusion | flops 455278592 | bytes 2949760 | tf_op jit(solution)/shard_map/flab,cb->flac/dot_general | solution.py:102
  59.8 2.1 %fusion.30 = f32[3,4,96,128]{3,2,1,0:T(8,128)S(1)} fusion(f32[3,4,96,128]{3,2,1,0:T(8,128)S(1)} %fusion, f32[1,4,96,512]{3,2,1,0:T(8,128)S(1)} %get-tuple-element.13, f32[1,4,96,512]{3,2,1,0:T(8,128)S(1)} %get-tuple-element.12, f32[1,4,96,512]{3,2,1,0:T(8,128)S(1)} %get-tuple-element.11, s32[512]{0:T(512)S(1)} %iota_add_fusion.2, s32[128]{0:T(128)S(1)} %mul.250, ...), kind=kOutput, calls=%fused_computation.31 | convolution fusion | flops 455426048 | bytes 3541632 | tf_op jit(solution)/shard_map/flab,cb->flac/dot_general | solution.py:102
  61.9 1.9 %fusion.27 = f32[3,4,96,128]{3,2,1,0:T(8,128)S(1)} fusion(f32[3,4,96,128]{3,2,1,0:T(8,128)S(1)} %fusion.30, f32[1,4,96,512]{3,2,1,0:T(8,128)S(1)} %get-tuple-element.10, f32[1,4,96,512]{3,2,1,0:T(8,128)S(1)} %get-tuple-element.9, f32[1,4,96,512]{3,2,1,0:T(8,128)S(1)} %get-tuple-element.8, s32[512]{0:T(512)S(1)} %iota_add_fusion.1, s32[128]{0:T(128)S(1)} %mul.250, ...), kind=kOutput, calls=%fused_computation.30 | convolution fusion | flops 455426048 | bytes 3541632 | tf_op jit(solution)/shard_map/flab,cb->flac/dot_general | solution.py:102
  63.8 1.9 %fusion.36 = bf16[3,4,96,128]{3,2,1,0:T(8,128)(2,1)S(1)} fusion(f32[3,4,96,128]{3,2,1,0:T(8,128)S(1)} %fusion.27, f32[1,4,96,512]{3,2,1,0:T(8,128)S(1)} %get-tuple-element.7, f32[1,4,96,512]{3,2,1,0:T(8,128)S(1)} %get-tuple-element.6, f32[1,4,96,512]{3,2,1,0:T(8,128)S(1)} %get-tuple-element.5, s32[512]{0:T(512)S(1)} %iota_add_fusion, s32[128]{0:T(128)S(1)} %mul.250, ...), kind=kOutput, calls=%fused_computation.33 | convolution fusion | flops 455720960 | bytes 3246720 | tf_op jit(solution)/shard_map/flab,cb->flac/dot_general | solution.py:102
  65.7 1.0 %copy.81 = bf16[3,4,96,128]{2,1,0,3:T(4,128)(2,1)} copy(bf16[3,4,96,128]{3,2,1,0:T(8,128)(2,1)S(1)} %fusion.36) | data formatting | bytes 589824 | tf_op jit(solution)/shard_map/convert_element_type | solution.py:109
  66.6 5.0 %all-to-all-start.1 = ((bf16[3,4,96,128]{2,1,0,3:T(4,128)(2,1)}), bf16[3,4,96,128]{2,1,0,3:T(4,128)(2,1)S(1)}, u32[]{:S(2)}, u32[]{:S(2)}) async-start(bf16[3,4,96,128]{2,1,0,3:T(4,128)(2,1)} %copy.81), calls=%async_computation.1 | async-start | bytes 786432 | tf_op jit(solution)/shard_map/all_to_all | solution.py:111
  71.8 9.2 %all-to-all-done.1 = bf16[3,4,96,128]{2,1,0,3:T(4,128)(2,1)S(1)} async-done(((bf16[3,4,96,128]{2,1,0,3:T(4,128)(2,1)}), bf16[3,4,96,128]{2,1,0,3:T(4,128)(2,1)S(1)}, u32[]{:S(2)}, u32[]{:S(2)}) %all-to-all-start.1) | async-done | bytes 294944 | tf_op jit(solution)/shard_map/all_to_all | solution.py:111
  82.9 6.2 %collective-permute-start = (bf16[3,2,2,4,65]{4,2,1,0,3:T(2,128)(2,1)S(1)}, bf16[3,2,2,4,65]{4,2,1,0,3:T(2,128)(2,1)S(1)}, u32[]{:S(2)}, u32[]{:S(2)}) collective-permute-start(bf16[3,2,2,4,65]{4,2,1,0,3:T(2,128)(2,1)S(1)} %get-tuple-element.19), channel_id=1, source_target_pairs={{0,1},{1,2},{2,3},{4,5},{5,6},{6,7},{8,9},{9,10},{10,11},{12,13},{... | collective-permute-start | bytes 18728 | tf_op jit(solution)/shard_map/ppermute | solution.py:22
  89.1 1.9 %collective-permute-start.1 = (bf16[3,2,2,4,65]{4,2,1,0,3:T(2,128)(2,1)S(1)}, bf16[3,2,2,4,65]{4,2,1,0,3:T(2,128)(2,1)S(1)}, u32[]{:S(2)}, u32[]{:S(2)}) collective-permute-start(bf16[3,2,2,4,65]{4,2,1,0,3:T(2,128)(2,1)S(1)} %get-tuple-element.20), channel_id=1, source_target_pairs={{1,0},{2,1},{3,2},{5,4},{6,5},{7,6},{9,8},{10,9},{11,10},{13,12},{... | collective-permute-start | bytes 18728 | tf_op jit(solution)/shard_map/ppermute | solution.py:24
  91.0 3.1 %collective-permute-done.1 = bf16[3,2,2,4,65]{4,2,1,0,3:T(2,128)(2,1)S(1)} collective-permute-done((bf16[3,2,2,4,65]{4,2,1,0,3:T(2,128)(2,1)S(1)}, bf16[3,2,2,4,65]{4,2,1,0,3:T(2,128)(2,1)S(1)}, u32[]{:S(2)}, u32[]{:S(2)}) %collective-permute-start.1) | collective-permute-done | bytes 6272 | tf_op jit(solution)/shard_map/ppermute | solution.py:24
  94.3 0.6 copy.88
  (60 shorter events, 6.7 us)
Async XLA Ops:
  0.0 2.3 %copy-start = (bf16[4,65,384]{2,0,1:T(4,128)(2,1)S(1)}, bf16[4,65,384]{2,0,1:T(4,128)(2,1)}, u32[]{:S(2)}) copy-start(bf16[4,65,384]{2,0,1:T(4,128)(2,1)} %param.8) | copy-start | bytes 599044
  9.1 13.3 %copy-start.5 = (u32[32]{0:T(128)S(1)}, u32[32]{0:T(128)}, u32[]{:S(2)}) copy-start(u32[32]{0:T(128)} %constant.104) | copy-start | bytes 388
  9.1 14.6 %copy-start.3 = (s32[4]{0:T(128)S(1)}, s32[4]{0:T(128)}, u32[]{:S(2)}) copy-start(s32[4]{0:T(128)} %param.9) | copy-start | bytes 52
  16.1 21.7 %all-to-all-start = ((bf16[8,2,18432]{2,1,0:T(2,128)(2,1)}), bf16[8,2,18432]{2,1,0:T(2,128)(2,1)S(1)}, u32[]{:S(2)}, u32[]{:S(2)}) async-start(bf16[8,2,18432]{2,1,0:T(2,128)(2,1)} %reshape.343), calls=%async_computation | async-start | bytes 1179648 | tf_op jit(solution)/shard_map/all_to_all | solution.py:93
  63.8 7.8 %copy-start.4 = (f32[16]{0:T(128)S(1)}, f32[16]{0:T(128)}, u32[]{:S(2)}) copy-start(f32[16]{0:T(128)} %param.11) | copy-start | bytes 196
  66.6 14.4 %all-to-all-start.1 = ((bf16[3,4,96,128]{2,1,0,3:T(4,128)(2,1)}), bf16[3,4,96,128]{2,1,0,3:T(4,128)(2,1)S(1)}, u32[]{:S(2)}, u32[]{:S(2)}) async-start(bf16[3,4,96,128]{2,1,0,3:T(4,128)(2,1)} %copy.81), calls=%async_computation.1 | async-start | bytes 786432 | tf_op jit(solution)/shard_map/all_to_all | solution.py:111
  81.2 1.1 %copy-start.2 = (f32[384]{0:T(512)S(1)}, f32[384]{0:T(512)}, u32[]{:S(2)}) copy-start(f32[384]{0:T(512)} %param.10) | copy-start | bytes 4612
  81.4 1.4 %copy-start.1 = (bf16[3,2,4,4,65]{4,3,2,1,0:T(4,128)(2,1)S(1)}, bf16[3,2,4,4,65]{4,3,2,1,0:T(4,128)(2,1)}, u32[]{:S(2)}) copy-start(bf16[3,2,4,4,65]{4,3,2,1,0:T(4,128)(2,1)} %param.6) | copy-start | bytes 37444
  82.9 8.1 %collective-permute-start = (bf16[3,2,2,4,65]{4,2,1,0,3:T(2,128)(2,1)S(1)}, bf16[3,2,2,4,65]{4,2,1,0,3:T(2,128)(2,1)S(1)}, u32[]{:S(2)}, u32[]{:S(2)}) collective-permute-start(bf16[3,2,2,4,65]{4,2,1,0,3:T(2,128)(2,1)S(1)} %get-tuple-element.19), channel_id=1, source_target_pairs={{0,1},{1,2},{2,3},{4,5},{5,6},{6,7},{8,9},{9,10},{10,11},{12,13},{... | collective-permute-start | bytes 18728 | tf_op jit(solution)/shard_map/ppermute | solution.py:22
  89.1 5.0 %collective-permute-start.1 = (bf16[3,2,2,4,65]{4,2,1,0,3:T(2,128)(2,1)S(1)}, bf16[3,2,2,4,65]{4,2,1,0,3:T(2,128)(2,1)S(1)}, u32[]{:S(2)}, u32[]{:S(2)}) collective-permute-start(bf16[3,2,2,4,65]{4,2,1,0,3:T(2,128)(2,1)S(1)} %get-tuple-element.20), channel_id=1, source_target_pairs={{1,0},{2,1},{3,2},{5,4},{6,5},{7,6},{9,8},{10,9},{11,10},{13,12},{... | collective-permute-start | bytes 18728 | tf_op jit(solution)/shard_map/ppermute | solution.py:24
where the time goes:
time: 95.6 us; the launch traced here: 95 us
  local copies, waits for them, and re-layouts  27.5 us (29%)
  starting transfers between devices  19.5 us (20%)
  matrix products  15.7 us (16%)
  blocking collectives  13.4 us (14%)
  waiting for transfers between devices  12.3 us (13%)
  other arithmetic  5.53 us (6%)
  between operations  1.06 us (1%)
    unnamed x1, blocking collectives  13.4 us
    unnamed x17, local copies, waits for them, and re-layouts  12.3 us
    all_to_all x1, waiting for transfers between devices, local(): lax.all_to_all(lamb_spec, 'ma', split_axis=3, concat_axis=2, tiled=True)  9.2 us
    dot_general x4, matrix products, local(): jnp.einsum('flab,cb->flac', lamb_vector, table_block.astype(jnp.float32),...  7.64 us
    dot_general x4, matrix products, local(): jnp.einsum('flac,cb->flab', spec_block, table_block, preferred_element_ty...  7.44 us
    all_to_all x1, starting transfers between devices, local(): lax.all_to_all(spectral, 'ma', split_axis=2, concat_axis=3, tiled=True)  6.37 us
    ppermute x1, starting transfers between devices, with_halo(): lax.ppermute(tail, axis, [(i, (i + 1) % count) for i in range(ends)])  6.19 us
    convert_element_type x2, local copies, waits for them, and re-layouts, local(): spectral.reshape(6, levels_dev, nlat_all, 4 * pair_count)  6.04 us
  transfers between devices with their start and end apart: 4, of which 2 were waited for; matrix products, arithmetic and copies ran while one was open for 1% of the time, Pallas kernels for 0%

commit v1 on v0

--- a/solution.py
+++ b/solution.py
@@ -1,8 +1,12 @@
+import functools
 import math
 
 import jax
 import jax.numpy as jnp
+import numpy as np
 from jax import lax
+from jax.experimental import pallas as pl
+from jax.experimental.pallas import tpu as pltpu
 from jax.sharding import PartitionSpec as P
 
 NLON = 2048
@@ -145,6 +149,301 @@
         1.0 + 2.0 * own_coupling
     )
 
+def lon_count(orders_all):
+    need = 3 * (orders_all - 1) + 1
+    return min(NLON, -(-need // 128) * 128)
+
+
+def pack_lanes(pair_count, pack_rows):
+    return -(-(pair_count * pack_rows + pair_count) // 128) * 128
+
+
+def remote(src, dst, send_sem, recv_sem, device_id):
+    return pltpu.make_async_remote_copy(
+        src_ref=src,
+        dst_ref=dst,
+        send_sem=send_sem,
+        recv_sem=recv_sem,
+        device_id=device_id,
+        device_id_type=pl.DeviceIdType.MESH,
+    )
+
+
+def fused_kernel(
+    n_ma, n_row, pairs, rows, levels,
+    coef_ref, leg_ref, weight_ref, dif_ref, tab_ref, tab_t_ref,
+    out_ref,
+    coef_all, leg_all, onehot, spec, wgt, part, part_in, ext,
+    coef_send, coef_recv, leg_send, leg_recv, part_send, part_recv, halo_send, halo_recv,
+):
+    me = lax.axis_index("ma")
+    row = lax.axis_index("row")
+    lanes = coef_ref.shape[1]
+    groups = coef_ref.shape[0]
+    fields2 = groups // 2
+    orders = rows - 1
+    slots = 2 * pairs
+    lat = leg_ref.shape[1]
+    used = pairs * rows
+    f32 = jnp.float32
+    bf16 = jnp.bfloat16
+    left = lax.rem(row + n_row - 1, n_row)
+    right = lax.rem(row + 1, n_row)
+
+    barrier = pltpu.get_barrier_semaphore()
+    for d in range(1, n_ma):
+        pl.semaphore_signal(
+            barrier, inc=1, device_id=(lax.rem(me + d, n_ma), row), device_id_type=pl.DeviceIdType.MESH
+        )
+    for side in (left, right):
+        pl.semaphore_signal(barrier, inc=1, device_id=(me, side), device_id_type=pl.DeviceIdType.MESH)
+    pl.semaphore_wait(barrier, n_ma + 1)
+
+    def coef_copy(d):
+        peer = lax.rem(me + d, n_ma)
+        return remote(coef_ref, coef_all.at[d], coef_send.at[d], coef_recv.at[d], (peer, row))
+
+    def leg_copy(d):
+        peer = lax.rem(me + d, n_ma)
+        return remote(leg_ref.at[peer], leg_all.at[d], leg_send.at[d], leg_recv.at[d], (peer, row))
+
+    for d in range(1, n_ma):
+        coef_copy(d).start()
+        leg_copy(d).start()
+
+    coef_all[0] = coef_ref[...]
+    leg_all[0] = leg_ref[me]
+
+    lane = lax.broadcasted_iota(jnp.int32, (slots, lanes), 1)
+    sub = lax.broadcasted_iota(jnp.int32, (slots, lanes), 0)
+    lane_pair = jnp.zeros((slots, lanes), jnp.int32)
+    for p in range(1, pairs):
+        lane_pair = lane_pair + (lane >= p * rows).astype(jnp.int32)
+    lane_row = lane - rows * lane_pair
+    own = (lane_pair == sub // 2) & (lane < used)
+    is_high = (sub % 2) == 1
+    m_lane = lax.broadcasted_iota(jnp.int32, (slots, orders), 1)
+    m_sub = lax.broadcasted_iota(jnp.int32, (slots, orders), 0)
+
+    def lows(d):
+        head = coef_all[d, 0:16, :].astype(f32)
+        return [head[0:1, used + p : used + p + 1].astype(jnp.int32) for p in range(pairs)]
+
+    def masks(d):
+        values = lows(d)
+        low = jnp.zeros((slots, lanes), jnp.int32)
+        for p in range(pairs):
+            low = jnp.where(lane_pair == p, values[p], low)
+        lower = lane_row < orders - low
+        picked = own & jnp.logical_xor(is_high, lower)
+        parity = jnp.where(is_high, lane_row + low, lane_row) & 1
+        even = (picked & (parity == 0)).astype(f32)
+        odd = (picked & (parity == 1)).astype(f32)
+        return even, odd
+
+    def synth(d, carry):
+        values = lows(d)
+        order = jnp.zeros((slots, orders), jnp.int32)
+        for p in range(pairs):
+            order = jnp.where(m_sub == 2 * p, values[p], order)
+            order = jnp.where(m_sub == 2 * p + 1, orders - 1 - values[p], order)
+        base = pl.multiple_of(d * slots, slots)
+        onehot[pl.ds(base, slots), :] = (m_lane == order).astype(f32)
+        even, odd = masks(d)
+        coef = coef_all[d].astype(f32)
+        leg = leg_all[d]
+        for h in range(2):
+            mask = even + odd if h == 0 else even - odd
+            lhs = (coef[:, None, :] * mask[None]).reshape(groups * slots, lanes).astype(bf16)
+            made = lax.dot_general(lhs, leg, (((1,), (1,)), ((), ())), preferred_element_type=f32)
+            spec[h, :, :, pl.ds(base, slots), :] = made.reshape(fields2, 2, slots, lat)
+        return carry
+
+    synth(0, 0)
+    def arrive(d, carry):
+        coef_copy(d).wait_recv()
+        leg_copy(d).wait_recv()
+        return synth(d, carry)
+    lax.fori_loop(1, n_ma, arrive, 0)
+
+    hot = onehot[...].astype(bf16)
+    full = n_ma * slots
+    to_grid = jnp.concatenate(
+        [
+            lax.dot_general(tab_t_ref[c], hot, (((1,), (1,)), ((), ())), preferred_element_type=f32)
+            for c in range(2)
+        ],
+        axis=1,
+    ).astype(bf16)
+    to_spec = jnp.concatenate(
+        [jnp.dot(hot, tab_ref[c], preferred_element_type=f32) for c in range(2)], axis=0
+    ).astype(bf16)
+    weight = weight_ref[...]
+
+    def middle(k, carry):
+        halves = []
+        for h in range(2):
+            grids = []
+            for g in range(2):
+                for f in range(3):
+                    block = spec[h, g * 3 * levels + k * 3 + f].reshape(2 * full, lat).astype(bf16)
+                    grids.append(jnp.dot(to_grid, block, preferred_element_type=f32))
+            u, w = grids[:3], grids[3:]
+            lamb = [
+                u[1] * w[2] - u[2] * w[1],
+                u[2] * w[0] - u[0] * w[2],
+                u[0] * w[1] - u[1] * w[0],
+            ]
+            halves.append(
+                [jnp.dot(to_spec, x.astype(bf16), preferred_element_type=f32) for x in lamb]
+            )
+        for f in range(3):
+            north, south = halves[0][f], halves[1][f]
+            wgt[0, k * 3 + f] = (weight * (north + south)).reshape(2, full, lat)
+            wgt[1, k * 3 + f] = (weight * (north - south)).reshape(2, full, lat)
+        return carry
+
+    lax.fori_loop(0, levels, middle, 0)
+
+    def part_copy(d):
+        peer = lax.rem(me + n_ma - d, n_ma)
+        return remote(part.at[d], part_in.at[d], part_send.at[d], part_recv.at[d], (peer, row))
+
+    def analyse(d):
+        base = pl.multiple_of(d * slots, slots)
+        total = None
+        for q, mask in enumerate(masks(d)):
+            lhs = wgt[q, :, :, pl.ds(base, slots), :].reshape(fields2 * slots, lat).astype(bf16)
+            made = jnp.dot(lhs, leg_all[d], preferred_element_type=f32)
+            made = made.reshape(fields2, slots, lanes) * mask[None]
+            total = made if total is None else total + made
+        return jnp.sum(total, axis=1)
+
+    def project(i, carry):
+        d = n_ma - i
+        part[d] = analyse(d).astype(bf16)
+        part_copy(d).start()
+        return carry
+
+    lax.fori_loop(1, n_ma, project, 0)
+    source = analyse(0) + coef_ref[0:fields2, :].astype(f32)
+
+    def gather(i, total):
+        d = n_ma - i
+        part_copy(d).wait_recv()
+        return total + part_in[d].astype(f32)
+
+    source = lax.fori_loop(1, n_ma, gather, source)
+    source = source.reshape(levels, fields2 // levels, lanes)
+    ext[2 : levels + 2] = source
+    to_left = remote(ext.at[2:4], ext.at[levels + 2 : levels + 4], halo_send.at[0], halo_recv.at[0], (me, left))
+    to_right = remote(ext.at[levels : levels + 2], ext.at[0:2], halo_send.at[1], halo_recv.at[1], (me, right))
+    to_left.start()
+    to_right.start()
+
+    def drain(d, carry):
+        coef_copy(d).wait_send()
+        leg_copy(d).wait_send()
+        part_copy(d).wait_send()
+        return carry
+
+    lax.fori_loop(1, n_ma, drain, 0)
+    to_left.wait()
+    to_right.wait()
+
+    shape = (fields2 // levels, lanes)
+    has_left = (row > 0).astype(f32)
+    has_right = (row < n_row - 1).astype(f32)
+    wide = [ext[i] for i in range(levels + 4)]
+    for i in range(2):
+        wide[i] = wide[i] * has_left
+        wide[levels + 2 + i] = wide[levels + 2 + i] * has_right
+    coupling = [jnp.full(shape, dif_ref[row * levels + i]) for i in range(levels + 4)]
+    inverse = [1.0 / (1.0 + 2.0 * c) for c in coupling]
+    first = [
+        (wide[i] + coupling[i] * (wide[i - 1] + wide[i + 1])) * inverse[i] for i in range(1, levels + 3)
+    ]
+    first[0] = first[0] * has_left
+    first[-1] = first[-1] * has_right
+    for k in range(levels):
+        done = (wide[k + 2] + coupling[k + 2] * (first[k] + first[k + 2])) * inverse[k + 2]
+        out_ref[k] = done[:, :used]
+
+
+def fused(velocity, vorticity, legendre, pair_order, lat_weight, diffusivity):
+    n_ma = lax.axis_size("ma")
+    n_row = lax.axis_size("row")
+    pairs, rows, half_lat = legendre.shape
+    levels = velocity.shape[2]
+    orders = rows - 1
+    used = pairs * rows
+    lanes = pack_lanes(pairs, rows)
+    lat = half_lat // n_ma
+    slots = 2 * pairs
+    full = n_ma * slots
+    points = lon_count(orders)
+    bf16 = jnp.bfloat16
+    f32 = jnp.float32
+
+    def packed(x):
+        return jnp.transpose(x, (2, 0, 1, 3, 4)).reshape(levels * 6, used)
+
+    groups = 12 * levels
+    coef = jnp.concatenate(
+        [
+            jnp.concatenate([packed(velocity), packed(vorticity)], axis=0),
+            jnp.broadcast_to(pair_order.astype(bf16)[None], (groups, pairs)),
+            jnp.zeros((groups, lanes - used - pairs), bf16),
+        ],
+        axis=1,
+    )
+    leg = jnp.transpose(legendre.reshape(used, half_lat))
+    leg = jnp.pad(leg, ((0, 0), (0, lanes - used))).reshape(n_ma, lat, lanes)
+    scale = (NLON / points) / math.sqrt(NLON) / orders
+    weight = lax.dynamic_slice_in_dim(lat_weight, lax.axis_index("ma") * lat, lat) * scale
+    angle = np.outer(np.arange(orders), np.arange(points)) % points * (2.0 * math.pi / points)
+    table = np.stack([np.cos(angle), -np.sin(angle)])
+    tab = jnp.asarray(table, bf16)
+    tab_t = jnp.asarray(np.transpose(table, (0, 2, 1)), bf16)
+    vmem = pl.BlockSpec(memory_space=pltpu.VMEM)
+    out = pl.pallas_call(
+        functools.partial(fused_kernel, n_ma, n_row, pairs, rows, levels),
+        out_shape=jax.ShapeDtypeStruct((levels, 6, used), f32),
+        in_specs=[vmem, vmem, vmem, pl.BlockSpec(memory_space=pltpu.SMEM), vmem, vmem],
+        out_specs=vmem,
+        scratch_shapes=[
+            pltpu.VMEM((n_ma, groups, lanes), bf16),
+            pltpu.VMEM((n_ma, lat, lanes), bf16),
+            pltpu.VMEM((full, orders), f32),
+            pltpu.VMEM((2, groups // 2, 2, full, lat), f32),
+            pltpu.VMEM((2, 3 * levels, 2, full, lat), f32),
+            pltpu.VMEM((n_ma, groups // 2, lanes), bf16),
+            pltpu.VMEM((n_ma, groups // 2, lanes), bf16),
+            pltpu.VMEM((levels + 4, 6, lanes), f32),
+        ]
+        + [pltpu.SemaphoreType.DMA((n_ma,))] * 6
+        + [pltpu.SemaphoreType.DMA((2,))] * 2,
+        compiler_params=pltpu.CompilerParams(
+            collective_id=0, has_side_effects=True, vmem_limit_bytes=48 * 1024 * 1024
+        ),
+    )(coef, leg, weight[None], jnp.pad(diffusivity, (2, 2)), tab, tab_t)
+    return jnp.transpose(out.reshape(levels, 3, 2, pairs, rows), (1, 2, 0, 3, 4))
+
+
+def fits(velocity, legendre):
+    n_ma = lax.axis_size("ma")
+    n_row = lax.axis_size("row")
+    pairs, rows, half_lat = legendre.shape
+    levels = velocity.shape[2]
+    small = rows <= 129 and pairs * n_ma <= 128 and half_lat // n_ma <= 128
+    whole = half_lat % n_ma == 0 and half_lat // n_ma % 16 == 0 and pairs % 4 == 0 and levels % 4 == 0
+    return small and whole and n_row > 2 and n_ma > 1
+
+
+def step(velocity, vorticity, legendre, pair_order, lat_weight, diffusivity):
+    chosen = fused if fits(velocity, legendre) else local
+    return chosen(velocity, vorticity, legendre, pair_order, lat_weight, diffusivity)
+
 
 def solution(mesh):
     in_specs = (
@@ -156,4 +455,4 @@
         P(),
     )
     out_specs = P(None, None, "row", "ma", None)
-    return jax.shard_map(local, mesh=mesh, in_specs=in_specs, out_specs=out_specs, check_vma=False)
+    return jax.shard_map(step, mesh=mesh, in_specs=in_specs, out_specs=out_specs, check_vma=False)

time: 95.6 us -> 38.7 us (0.40)
  Pallas kernels: 0 us -> 33.3 us
  local copies, waits for them, and re-layouts: 27.5 us -> 4.29 us
  starting transfers between devices: 19.5 us -> 0 us
  matrix products: 15.7 us -> 0 us
  blocking collectives: 13.4 us -> 0 us
  waiting for transfers between devices: 12.3 us -> 0 us
  other arithmetic: 5.53 us -> 0.77 us
  between operations: 1.06 us -> 0.1 us
    pallas_call x0 -> x1, Pallas kernels: none -> 33.3 us  [fused(): pl.pallas_call(functools.partial(fused_kernel, n_ma, n_row, pairs, rows,...]
    dot_general x10 -> x0, matrix products: 15.7 us -> none  [the longest x4 7.64 us: local(): jnp.einsum('flab,cb->flac', lamb_vector, table_block.astype(jnp.float32),...]
    unnamed x1 -> x0, blocking collectives: 13.4 us -> none
    all_to_all x2 -> x0, starting transfers between devices: 11.3 us -> none  [the longest x1 6.37 us: local(): lax.all_to_all(spectral, 'ma', split_axis=2, concat_axis=3, tiled=True)]
    unnamed x17 -> x14, local copies, waits for them, and re-layouts: 12.3 us -> 3.03 us
    all_to_all x2 -> x0, waiting for transfers between devices: 9.2 us -> none  [the longest x1 9.2 us: local(): lax.all_to_all(lamb_spec, 'ma', split_axis=3, concat_axis=2, tiled=True)]
    ppermute x2 -> x0, starting transfers between devices: 8.11 us -> none  [the longest x1 6.19 us: with_halo(): lax.ppermute(tail, axis, [(i, (i + 1) % count) for i in range(ends)])]
    convert_element_type x4 -> x0, local copies, waits for them, and re-layouts: 7.01 us -> none  [the longest x2 6.04 us: local(): spectral.reshape(6, levels_dev, nlat_all, 4 * pair_count)]
  transfers between devices with their start and end apart: 4 -> 0, of which waited for: 2 -> 0; matrix products, arithmetic and copies ran while one was open for 1% -> 0% of each run, Pallas kernels for 0% -> 0%
where the time goes in v1:
time: 38.7 us; the launch traced here: 38.4 us
  Pallas kernels  33.3 us (86%)
  local copies, waits for them, and re-layouts  4.29 us (11%)
  other arithmetic  0.77 us (2%)
    pallas_call x1, Pallas kernels, fused(): pl.pallas_call(functools.partial(fused_kernel, n_ma, n_row, pairs, rows,...  33.3 us
    unnamed x14, local copies, waits for them, and re-layouts  3.03 us

profile of v1, /device:TPU:1, one launch (start us, length us, event | category | flops | bytes accessed | tf_op | source)
XLA Modules:
  0.0 38.4 jit_solution(17062866200538380536)
XLA Ops:
  0.0 0.8 %multiply_bitcast_fusion.weight_ref = f32[1,48]{1,0:T(1,128)S(1)} fusion(f32[384]{0:T(512)} %param.12, s32[]{:T(128)S(6)} %select_n.3), kind=kLoop, calls=%fused_computation.1 | loop fusion | flops 48 | bytes 388 | tf_op jit(solution)/shard_map/broadcast_in_dim | solution.py:429
  0.8 1.0 %copy.14 = bf16[4,65,384]{2,1,0:T(8,128)(2,1)S(1)} copy(bf16[4,65,384]{2,0,1:T(4,128)(2,1)} %param.10) | data formatting | bytes 399360 | tf_op args[2]
  1.7 0.1 reshape.18
  1.8 0.2 copy.17
  2.0 0.0 copy-start.2
  2.0 0.0 copy-start.3
  2.1 0.7 %copy-done.2 = bf16[3,2,4,4,65]{4,3,2,1,0:T(4,128)(2,1)S(1)} copy-done((bf16[3,2,4,4,65]{4,3,2,1,0:T(4,128)(2,1)S(1)}, bf16[3,2,4,4,65]{4,3,2,1,0:T(4,128)(2,1)}, u32[]{:S(2)}) %copy-start.2) | copy-done | bytes 12504
  2.7 0.0 copy-start
  2.8 0.1 reshape.16
  2.9 0.0 copy-done.3
  2.9 0.0 copy-start.4
  2.9 0.0 copy-start.1
  2.9 0.1 reshape.17
  3.0 0.5 %copy-done.4 = s32[4]{0:T(128)S(1)} copy-done((s32[4]{0:T(128)S(1)}, s32[4]{0:T(128)}, u32[]{:S(2)}) %copy-start.4) | copy-done | bytes 40
  3.5 0.1 pad.12.clone
  3.6 0.1 pad.13.clone
  3.7 0.0 copy-start.5
  3.7 0.6 %copy-done.5 = f32[16]{0:T(128)S(1)} copy-done((f32[16]{0:T(128)S(1)}, f32[16]{0:T(128)}, u32[]{:S(2)}) %copy-start.5) | copy-done | bytes 88
  4.3 0.1 pad.9.dif_ref
  4.4 0.0 copy-done
  4.4 0.0 copy-done.1
  4.4 33.3 %shard_map.82 = f32[4,6,260]{2,1,0:T(8,128)S(1)} custom-call(bf16[48,384]{1,0:T(8,128)(2,1)S(1)} %maximum_maximum_fusion.coef_ref, bf16[8,48,384]{2,1,0:T(8,128)(2,1)S(1)} %bitcast.9, f32[1,48]{1,0:T(1,128)S(1)} %multiply_bitcast_fusion.weight_ref, f32[20]{0:T(128)S(1)} %pad.9.dif_ref, bf16[2,64,256]{2,1,0:T(8,128)(2,1)S(1)} %copy-done.1, ...), custom_call_target="tpu_custom_call" | custom-call | tf_op jit(solution)/shard_map/pallas_call | solution.py:409
  37.7 0.7 %reshape.20 = f32[4,3,2,4,65]{4,3,0,2,1:T(4,128)} reshape(f32[4,6,260]{2,0,1:T(4,128)S(1)} %copy.16) | data formatting | bytes 49920 | tf_op jit(solution)/shard_map/reshape | solution.py:430
  (7 shorter events, 0.1 us)
Async XLA Ops:
  2.0 0.7 %copy-start.2 = (bf16[3,2,4,4,65]{4,3,2,1,0:T(4,128)(2,1)S(1)}, bf16[3,2,4,4,65]{4,3,2,1,0:T(4,128)(2,1)}, u32[]{:S(2)}) copy-start(bf16[3,2,4,4,65]{4,3,2,1,0:T(4,128)(2,1)} %param.8) | copy-start | bytes 37444
  2.0 0.8 %copy-start.3 = (bf16[3,2,4,4,65]{4,3,2,1,0:T(4,128)(2,1)S(1)}, bf16[3,2,4,4,65]{4,3,2,1,0:T(4,128)(2,1)}, u32[]{:S(2)}) copy-start(bf16[3,2,4,4,65]{4,3,2,1,0:T(4,128)(2,1)} %param.9) | copy-start | bytes 37444
  2.7 1.7 %copy-start = (bf16[2,256,64]{2,1,0:T(8,128)(2,1)S(1)}, bf16[2,256,64]{2,1,0:T(8,128)(2,1)}, u32[]{:S(2)}) copy-start(bf16[2,256,64]{2,1,0:T(8,128)(2,1)} %constant.24.clone.tab_t_ref) | copy-start | bytes 196612
  2.9 0.7 %copy-start.4 = (s32[4]{0:T(128)S(1)}, s32[4]{0:T(128)}, u32[]{:S(2)}) copy-start(s32[4]{0:T(128)} %param.11) | copy-start | bytes 52
  2.9 1.5 %copy-start.1 = (bf16[2,64,256]{2,1,0:T(8,128)(2,1)S(1)}, bf16[2,64,256]{2,1,0:T(8,128)(2,1)}, u32[]{:S(2)}) copy-start(bf16[2,64,256]{2,1,0:T(8,128)(2,1)} %constant.23.clone.tab_ref) | copy-start | bytes 196612
  3.7 0.7 %copy-start.5 = (f32[16]{0:T(128)S(1)}, f32[16]{0:T(128)}, u32[]{:S(2)}) copy-start(f32[16]{0:T(128)} %param.13) | copy-start | bytes 196

commit v2 on v1

--- a/solution.py
+++ b/solution.py
@@ -154,10 +154,6 @@
     return min(NLON, -(-need // 128) * 128)
 
 
-def pack_lanes(pair_count, pack_rows):
-    return -(-(pair_count * pack_rows + pair_count) // 128) * 128
-
-
 def remote(src, dst, send_sem, recv_sem, device_id):
     return pltpu.make_async_remote_copy(
         src_ref=src,
@@ -171,22 +167,34 @@
 
 def fused_kernel(
     n_ma, n_row, pairs, rows, levels,
-    coef_ref, leg_ref, weight_ref, dif_ref, tab_ref, tab_t_ref,
+    coef_ref, leg_ref, rest_ref, weight_ref, dif_ref, tab_ref, tab_t_ref,
     out_ref,
-    coef_all, leg_all, onehot, spec, wgt, part, part_in, ext,
-    coef_send, coef_recv, leg_send, leg_recv, part_send, part_recv, halo_send, halo_recv,
+    coef_all, leg_all, rest_all, rest_t, onehot, spec, wgt, part, part_in, ext,
+    coef_send, coef_recv, leg_send, leg_recv, swap_send, swap_recv, rest_send, rest_recv, part_send, part_recv, halo_send, halo_recv,
 ):
     me = lax.axis_index("ma")
     row = lax.axis_index("row")
-    lanes = coef_ref.shape[1]
-    groups = coef_ref.shape[0]
+    chunks, groups, wide_lanes = coef_ref.shape
+    lanes = (chunks + 1) * wide_lanes
     fields2 = groups // 2
     orders = rows - 1
     slots = 2 * pairs
-    lat = leg_ref.shape[1]
-    used = pairs * rows
+    lat = leg_ref.shape[2]
+    main = pairs * orders
     f32 = jnp.float32
     bf16 = jnp.bfloat16
+    n_z = n_ma // 2
+    z, y = me // 2, lax.rem(me, 2)
+    mate = me + 1 - 2 * y
+    half = lax.rem(row, 2)
+    mate_row = row + 1 - 2 * half
+
+    def target(s):
+        return lax.rem(z + s // 2, n_z) * 2 + lax.rem(y + lax.rem(s, 2), 2)
+
+    def origin(s):
+        return lax.rem(z + n_z - s // 2, n_z) * 2 + lax.rem(y + lax.rem(s, 2), 2)
+
     left = lax.rem(row + n_row - 1, n_row)
     right = lax.rem(row + 1, n_row)
 
@@ -199,38 +207,57 @@
         pl.semaphore_signal(barrier, inc=1, device_id=(me, side), device_id_type=pl.DeviceIdType.MESH)
     pl.semaphore_wait(barrier, n_ma + 1)
 
-    def coef_copy(d):
-        peer = lax.rem(me + d, n_ma)
-        return remote(coef_ref, coef_all.at[d], coef_send.at[d], coef_recv.at[d], (peer, row))
-
-    def leg_copy(d):
-        peer = lax.rem(me + d, n_ma)
-        return remote(leg_ref.at[peer], leg_all.at[d], leg_send.at[d], leg_recv.at[d], (peer, row))
-
-    for d in range(1, n_ma):
-        coef_copy(d).start()
-        leg_copy(d).start()
+    def coef_copy(s):
+        if s % 2 == 0:
+            return remote(coef_ref, coef_all.at[s], coef_send.at[s], coef_recv.at[s], (target(s), row))
+        src = coef_ref if s == 1 else coef_all.at[s - 1]
+        return remote(src, coef_all.at[s], coef_send.at[s], coef_recv.at[s], (mate, row))
+
+    def leg_copy(s):
+        peer = target(s)
+        return remote(
+            leg_ref.at[peer, half], leg_all.at[s, half], leg_send.at[s], leg_recv.at[s], (peer, row)
+        )
+
+    def swap_copy(s):
+        return remote(
+            leg_all.at[s, half], leg_all.at[s, half], swap_send.at[s], swap_recv.at[s], (me, mate_row)
+        )
+
+    def rest_copy(s):
+        peer = target(s)
+        return remote(rest_ref.at[peer], rest_all.at[s], rest_send.at[s], rest_recv.at[s], (peer, row))
+
+    for s in range(1, n_ma):
+        rest_copy(s).start()
+    for s in range(n_ma - 2, 0, -2):
+        coef_copy(s).start()
+        leg_copy(s).start()
+        leg_copy(s + 1).start()
+    coef_copy(1).start()
+    leg_copy(1).start()
 
     coef_all[0] = coef_ref[...]
     leg_all[0] = leg_ref[me]
+    rest_all[0] = rest_ref[me]
 
     lane = lax.broadcasted_iota(jnp.int32, (slots, lanes), 1)
     sub = lax.broadcasted_iota(jnp.int32, (slots, lanes), 0)
-    lane_pair = jnp.zeros((slots, lanes), jnp.int32)
-    for p in range(1, pairs):
-        lane_pair = lane_pair + (lane >= p * rows).astype(jnp.int32)
-    lane_row = lane - rows * lane_pair
-    own = (lane_pair == sub // 2) & (lane < used)
     is_high = (sub % 2) == 1
     m_lane = lax.broadcasted_iota(jnp.int32, (slots, orders), 1)
     m_sub = lax.broadcasted_iota(jnp.int32, (slots, orders), 0)
 
     def lows(d):
-        head = coef_all[d, 0:16, :].astype(f32)
-        return [head[0:1, used + p : used + p + 1].astype(jnp.int32) for p in range(pairs)]
+        tile = rest_all[d].astype(jnp.float32)
+        return [tile[pairs + p : pairs + p + 1, 0:1].astype(jnp.int32) for p in range(pairs)]
 
     def masks(d):
         values = lows(d)
+        extra = lane - main - 8 * d
+        in_main = lane < main
+        lane_pair = jnp.where(in_main, lane // orders, extra)
+        lane_row = jnp.where(in_main, lane % orders, orders)
+        own = lane_pair == sub // 2
         low = jnp.zeros((slots, lanes), jnp.int32)
         for p in range(pairs):
             low = jnp.where(lane_pair == p, values[p], low)
@@ -241,6 +268,10 @@
         odd = (picked & (parity == 1)).astype(f32)
         return even, odd
 
+    def leg_of(d):
+        tail = rest_t[wide_lanes // 2 : wide_lanes // 2 + lat, :].astype(bf16)
+        return jnp.concatenate([leg_all[d, c] for c in range(chunks)] + [tail], axis=1)
+
     def synth(d, carry):
         values = lows(d)
         order = jnp.zeros((slots, orders), jnp.int32)
@@ -250,8 +281,10 @@
         base = pl.multiple_of(d * slots, slots)
         onehot[pl.ds(base, slots), :] = (m_lane == order).astype(f32)
         even, odd = masks(d)
-        coef = coef_all[d].astype(f32)
-        leg = leg_all[d]
+        coef = jnp.concatenate(
+            [coef_all[d, c].astype(f32) for c in range(chunks)] + [rest_t[0:groups, :]], axis=1
+        )
+        leg = leg_of(d)
         for h in range(2):
             mask = even + odd if h == 0 else even - odd
             lhs = (coef[:, None, :] * mask[None]).reshape(groups * slots, lanes).astype(bf16)
@@ -259,12 +292,27 @@
             spec[h, :, :, pl.ds(base, slots), :] = made.reshape(fields2, 2, slots, lat)
         return carry
 
+    for s in range(1, n_ma):
+        rest_copy(s).wait_recv()
+    rest = rest_all[...].astype(f32).reshape(n_ma * 8, wide_lanes)
+    rest = jnp.concatenate([rest, jnp.zeros((wide_lanes - n_ma * 8, wide_lanes), f32)], axis=0)
+    rest_t[...] = jnp.transpose(rest)
+    leg_copy(1).wait_recv()
+    swap_copy(1).start()
+    for s in range(2, n_ma, 2):
+        coef_copy(s).wait_recv()
+        coef_copy(s + 1).start()
+        for t in (s, s + 1):
+            leg_copy(t).wait_recv()
+            swap_copy(t).start()
     synth(0, 0)
-    def arrive(d, carry):
-        coef_copy(d).wait_recv()
-        leg_copy(d).wait_recv()
-        return synth(d, carry)
-    lax.fori_loop(1, n_ma, arrive, 0)
+    for s in range(1, n_ma):
+        if s % 2 == 1:
+            coef_copy(s).wait_recv()
+        remote(
+            leg_all.at[s, half], leg_all.at[s, 1 - half], swap_send.at[s], swap_recv.at[s], (me, mate_row)
+        ).wait_recv()
+        synth(s, 0)
 
     hot = onehot[...].astype(bf16)
     full = n_ma * slots
@@ -306,15 +354,14 @@
     lax.fori_loop(0, levels, middle, 0)
 
     def part_copy(d):
-        peer = lax.rem(me + n_ma - d, n_ma)
-        return remote(part.at[d], part_in.at[d], part_send.at[d], part_recv.at[d], (peer, row))
+        return remote(part.at[d], part_in.at[d], part_send.at[d], part_recv.at[d], (origin(d), row))
 
     def analyse(d):
         base = pl.multiple_of(d * slots, slots)
         total = None
         for q, mask in enumerate(masks(d)):
             lhs = wgt[q, :, :, pl.ds(base, slots), :].reshape(fields2 * slots, lat).astype(bf16)
-            made = jnp.dot(lhs, leg_all[d], preferred_element_type=f32)
+            made = jnp.dot(lhs, leg_of(d), preferred_element_type=f32)
             made = made.reshape(fields2, slots, lanes) * mask[None]
             total = made if total is None else total + made
         return jnp.sum(total, axis=1)
@@ -326,7 +373,7 @@
         return carry
 
     lax.fori_loop(1, n_ma, project, 0)
-    source = analyse(0) + coef_ref[0:fields2, :].astype(f32)
+    source = analyse(0)
 
     def gather(i, total):
         d = n_ma - i
@@ -334,6 +381,12 @@
         return total + part_in[d].astype(f32)
 
     source = lax.fori_loop(1, n_ma, gather, source)
+    tail = source[:, main:]
+    for shift in (8, 16, 32):
+        tail = tail + pltpu.roll(tail, wide_lanes - shift, 1)
+    own_tail = rest_t[0:fields2, :]
+    heads = [source[:, c * wide_lanes : (c + 1) * wide_lanes] + coef_ref[c, 0:fields2].astype(f32) for c in range(chunks)]
+    source = jnp.concatenate(heads + [tail + own_tail], axis=1)
     source = source.reshape(levels, fields2 // levels, lanes)
     ext[2 : levels + 2] = source
     to_left = remote(ext.at[2:4], ext.at[levels + 2 : levels + 4], halo_send.at[0], halo_recv.at[0], (me, left))
@@ -341,13 +394,12 @@
     to_left.start()
     to_right.start()
 
-    def drain(d, carry):
-        coef_copy(d).wait_send()
-        leg_copy(d).wait_send()
-        part_copy(d).wait_send()
-        return carry
-
-    lax.fori_loop(1, n_ma, drain, 0)
+    for s in range(1, n_ma):
+        coef_copy(s).wait_send()
+        leg_copy(s).wait_send()
+        swap_copy(s).wait_send()
+        rest_copy(s).wait_send()
+        part_copy(s).wait_send()
     to_left.wait()
     to_right.wait()
 
@@ -367,7 +419,7 @@
     first[-1] = first[-1] * has_right
     for k in range(levels):
         done = (wide[k + 2] + coupling[k + 2] * (first[k] + first[k + 2])) * inverse[k + 2]
-        out_ref[k] = done[:, :used]
+        out_ref[k] = done[:, : main + pairs]
 
 
 def fused(velocity, vorticity, legendre, pair_order, lat_weight, diffusivity):
@@ -376,29 +428,32 @@
     pairs, rows, half_lat = legendre.shape
     levels = velocity.shape[2]
     orders = rows - 1
-    used = pairs * rows
-    lanes = pack_lanes(pairs, rows)
+    main = pairs * orders
+    used = main + pairs
+    chunks = main // 128
+    lanes = main + 128
     lat = half_lat // n_ma
     slots = 2 * pairs
     full = n_ma * slots
     points = lon_count(orders)
     bf16 = jnp.bfloat16
     f32 = jnp.float32
-
-    def packed(x):
-        return jnp.transpose(x, (2, 0, 1, 3, 4)).reshape(levels * 6, used)
-
     groups = 12 * levels
-    coef = jnp.concatenate(
-        [
-            jnp.concatenate([packed(velocity), packed(vorticity)], axis=0),
-            jnp.broadcast_to(pair_order.astype(bf16)[None], (groups, pairs)),
-            jnp.zeros((groups, lanes - used - pairs), bf16),
-        ],
-        axis=1,
-    )
-    leg = jnp.transpose(legendre.reshape(used, half_lat))
-    leg = jnp.pad(leg, ((0, 0), (0, lanes - used))).reshape(n_ma, lat, lanes)
+    heads, tails = [], []
+    for x in (velocity, vorticity):
+        x = jnp.transpose(x, (2, 0, 1, 3, 4))
+        heads.append(x[..., :orders].reshape(6 * levels, chunks, 128))
+        tails.append(x[..., orders].reshape(6 * levels, pairs))
+    coef = jnp.transpose(jnp.concatenate(heads, axis=0), (1, 0, 2))
+    leg = legendre[:, :orders].reshape(chunks, 128, n_ma, lat)
+    leg = jnp.transpose(leg, (2, 0, 3, 1))
+    coef_tail = jnp.transpose(jnp.concatenate(tails, axis=0))
+    coef_tail = jnp.pad(coef_tail, ((0, 0), (0, 64 - groups)))
+    leg_tail = jnp.transpose(legendre[:, orders].reshape(pairs, n_ma, lat), (1, 0, 2))
+    leg_tail = jnp.pad(leg_tail, ((0, 0), (0, 0), (0, 64 - lat)))
+    tail = jnp.concatenate([jnp.broadcast_to(coef_tail, (n_ma, pairs, 64)), leg_tail], axis=2)
+    order_rows = jnp.broadcast_to(pair_order.astype(bf16)[None, :, None], (n_ma, pairs, 128))
+    rest = jnp.concatenate([tail, order_rows], axis=1)
     scale = (NLON / points) / math.sqrt(NLON) / orders
     weight = lax.dynamic_slice_in_dim(lat_weight, lax.axis_index("ma") * lat, lat) * scale
     angle = np.outer(np.arange(orders), np.arange(points)) % points * (2.0 * math.pi / points)
@@ -409,11 +464,13 @@
     out = pl.pallas_call(
         functools.partial(fused_kernel, n_ma, n_row, pairs, rows, levels),
         out_shape=jax.ShapeDtypeStruct((levels, 6, used), f32),
-        in_specs=[vmem, vmem, vmem, pl.BlockSpec(memory_space=pltpu.SMEM), vmem, vmem],
+        in_specs=[vmem, vmem, vmem, vmem, pl.BlockSpec(memory_space=pltpu.SMEM), vmem, vmem],
         out_specs=vmem,
         scratch_shapes=[
-            pltpu.VMEM((n_ma, groups, lanes), bf16),
-            pltpu.VMEM((n_ma, lat, lanes), bf16),
+            pltpu.VMEM((n_ma, chunks, groups, 128), bf16),
+            pltpu.VMEM((n_ma, chunks, lat, 128), bf16),
+            pltpu.VMEM((n_ma, 8, 128), bf16),
+            pltpu.VMEM((128, 128), f32),
             pltpu.VMEM((full, orders), f32),
             pltpu.VMEM((2, groups // 2, 2, full, lat), f32),
             pltpu.VMEM((2, 3 * levels, 2, full, lat), f32),
@@ -421,12 +478,15 @@
             pltpu.VMEM((n_ma, groups // 2, lanes), bf16),
             pltpu.VMEM((levels + 4, 6, lanes), f32),
         ]
-        + [pltpu.SemaphoreType.DMA((n_ma,))] * 6
+        + [pltpu.SemaphoreType.DMA((n_ma,))] * 10
         + [pltpu.SemaphoreType.DMA((2,))] * 2,
         compiler_params=pltpu.CompilerParams(
             collective_id=0, has_side_effects=True, vmem_limit_bytes=48 * 1024 * 1024
         ),
-    )(coef, leg, weight[None], jnp.pad(diffusivity, (2, 2)), tab, tab_t)
+    )(coef, leg, rest, weight[None], jnp.pad(diffusivity, (2, 2)), tab, tab_t)
+    out = jnp.concatenate(
+        [out[..., :main].reshape(levels, 6, pairs, orders), out[..., main:, None]], axis=3
+    )
     return jnp.transpose(out.reshape(levels, 3, 2, pairs, rows), (1, 2, 0, 3, 4))
 
 
@@ -435,9 +495,10 @@
     n_row = lax.axis_size("row")
     pairs, rows, half_lat = legendre.shape
     levels = velocity.shape[2]
-    small = rows <= 129 and pairs * n_ma <= 128 and half_lat // n_ma <= 128
-    whole = half_lat % n_ma == 0 and half_lat // n_ma % 16 == 0 and pairs % 4 == 0 and levels % 4 == 0
-    return small and whole and n_row > 2 and n_ma > 1
+    lat = half_lat // n_ma
+    tiles = pairs == 4 and pairs * (rows - 1) == 256 and n_ma % 2 == 0 and n_ma <= 8 and n_row % 2 == 0
+    whole = half_lat % n_ma == 0 and lat % 16 == 0 and lat <= 64 and levels == 4
+    return tiles and whole and n_row > 2 and n_ma > 1
 
 
 def step(velocity, vorticity, legendre, pair_order, lat_weight, diffusivity):

time: 38.7 us -> 35.3 us (0.912)
  Pallas kernels: 33.3 us -> 27.9 us
  local copies, waits for them, and re-layouts: 4.29 us -> 5.23 us
  other arithmetic: 0.77 us -> 1.67 us
    pallas_call x1, Pallas kernels: 33.3 us -> 27.9 us  [fused(): pl.pallas_call(functools.partial(fused_kernel, n_ma, n_row, pairs, rows,...]
    slice x0 -> x15, local copies, waits for them, and re-layouts: none -> 3.36 us  [the longest x3 1.21 us: fused(): leg = legendre[:, :orders].reshape(chunks, 128, n_ma, lat)]
    unnamed x14 -> x12, local copies, waits for them, and re-layouts: 3.03 us -> 0.66 us
    transpose x0 -> x3, other arithmetic: none -> 0.8 us  [the longest x1 0.72 us: fused(): jnp.transpose(out.reshape(levels, 3, 2, pairs, rows), (1, 2, 0, 3, 4))]
    reshape x4 -> x6, local copies, waits for them, and re-layouts: 0.96 us -> 0.42 us  [the longest x2 0.23 us: fused(): leg = legendre[:, :orders].reshape(chunks, 128, n_ma, lat)]
where the time goes in v2:
time: 35.3 us; the launch traced here: 35 us
  Pallas kernels  27.9 us (79%)
  local copies, waits for them, and re-layouts  5.23 us (15%)
  other arithmetic  1.67 us (5%)
    pallas_call x1, Pallas kernels, fused(): pl.pallas_call(functools.partial(fused_kernel, n_ma, n_row, pairs, rows,...  27.9 us
    slice x3, local copies, waits for them, and re-layouts, fused(): leg = legendre[:, :orders].reshape(chunks, 128, n_ma, lat)  1.21 us
    broadcast_in_dim x1, other arithmetic, fused(): weight[None]  0.76 us
    slice x2, local copies, waits for them, and re-layouts, fused(): heads.append(x[..., :orders].reshape(6 * levels, chunks, 128))  0.76 us
    transpose x1, other arithmetic, fused(): jnp.transpose(out.reshape(levels, 3, 2, pairs, rows), (1, 2, 0, 3, 4))  0.72 us

profile of v2, /device:TPU:1, one launch (start us, length us, event | category | flops | bytes accessed | tf_op | source)
XLA Modules:
  0.0 35.0 jit_solution(16362039452651377324)
XLA Ops:
  0.0 0.7 %copy.29 = bf16[4,3,2,4,64]{4,3,2,1,0:T(4,128)(2,1)S(1)} copy(bf16[4,3,2,4,64]{4,3,0,2,1:T(4,128)(2,1)} %bitcast.28) | data formatting | bytes 24576 | tf_op jit(solution)/shard_map/slice | solution.py:445
  0.8 0.1 reshape.17
  0.9 0.6 %copy-done.3 = bf16[3,2,4,4,65]{4,3,2,1,0:T(4,128)(2,1)S(1)} copy-done((bf16[3,2,4,4,65]{4,3,2,1,0:T(4,128)(2,1)S(1)}, bf16[3,2,4,4,65]{4,3,2,1,0:T(4,128)(2,1)}, u32[]{:S(2)}) %copy-start.3) | copy-done | bytes 12504
  1.5 0.1 reshape.16
  1.6 0.9 %slice-done = bf16[4,64,384]{2,0,1:T(4,128)(2,1)S(1)} async-done(((bf16[4,65,384]{2,0,1:T(4,128)(2,1)}), bf16[4,64,384]{2,0,1:T(4,128)(2,1)S(1)}, s32[]{:S(2)}) %slice-start) | async-done | bytes 196632 | tf_op jit(solution)/shard_map/slice | solution.py:448
  2.5 0.3 copy.32
  2.8 0.2 reshape.18
  3.1 0.7 %slice-done.1 = bf16[4,1,384]{2,0,1:T(4,128)(2,1)S(1)} async-done(((bf16[4,65,384]{2,0,1:T(4,128)(2,1)}), bf16[4,1,384]{2,0,1:T(4,128)(2,1)S(1)}, s32[]{:S(2)}) %slice-start.1) | async-done | bytes 3096 | tf_op jit(solution)/shard_map/slice | solution.py:452
  3.8 0.1 reshape_squeeze.11
  3.9 0.1 pad.19.clone
  4.0 0.1 slice.35
  4.1 0.3 copy.35
  4.3 0.1 copy.37
  4.4 0.1 slice.34
  4.5 0.3 copy.34
  4.8 0.1 copy.36
  4.9 0.1 maximum_bitcast_fusion.2
  5.0 0.1 fusion.4.rest_ref
  5.1 0.8 %multiply_bitcast_fusion.weight_ref = f32[1,48]{1,0:T(1,128)S(1)} fusion(f32[384]{0:T(512)} %param.12, s32[]{:T(128)S(6)} %select_n.3), kind=kLoop, calls=%fused_computation.17 | loop fusion | flops 48 | bytes 388 | tf_op jit(solution)/shard_map/broadcast_in_dim | solution.py:486
  5.9 0.1 pad.14.dif_ref
  5.9 27.9 %shard_map.82 = f32[4,6,260]{2,1,0:T(8,128)S(1)} custom-call(bf16[2,48,128]{2,1,0:T(8,128)(2,1)S(1)} %maximum_bitcast_fusion.1.coef_ref, bf16[8,2,48,128]{3,2,1,0:T(8,128)(2,1)S(1)} %bitcast.27, bf16[8,8,128]{2,1,0:T(8,128)(2,1)S(1)} %fusion.4.rest_ref, f32[1,48]{1,0:T(1,128)S(1)} %multiply_bitcast_fusion.weight_ref, f32[20]{0:T(128)S(1)} %pad.14.dif_ref, ...), custom_call_target="tpu_custom_call" | custom-call | tf_op jit(solution)/shard_map/pallas_call | solution.py:464
  33.9 0.3 copy.41
  34.2 0.1 concatenate.24
  34.3 0.7 %maximum_bitcast_fusion = f32[3,2,4,4,65]{4,3,2,1,0:T(4,128)} fusion(f32[4,3,2,4,1]{4,3,0,2,1:T(4,128)S(1)} %copy.41, f32[4,3,2,4,64]{4,3,0,2,1:T(4,128)S(1)} %concatenate.24), kind=kLoop, calls=%fused_computation.1 | loop fusion | flops 6240 | bytes 49920 | tf_op jit(solution)/shard_map/transpose | solution.py:490
  (25 shorter events, 0.2 us)
Async XLA Ops:
  0.8 0.7 %copy-start.3 = (bf16[3,2,4,4,65]{4,3,2,1,0:T(4,128)(2,1)S(1)}, bf16[3,2,4,4,65]{4,3,2,1,0:T(4,128)(2,1)}, u32[]{:S(2)}) copy-start(bf16[3,2,4,4,65]{4,3,2,1,0:T(4,128)(2,1)} %param.8) | copy-start | bytes 37444
  1.6 0.9 %slice-start = ((bf16[4,65,384]{2,0,1:T(4,128)(2,1)}), bf16[4,64,384]{2,0,1:T(4,128)(2,1)S(1)}, s32[]{:S(2)}) async-start(bf16[4,65,384]{2,0,1:T(4,128)(2,1)} %param.10), calls=%async_computation | async-start | bytes 393216 | tf_op jit(solution)/shard_map/slice | solution.py:448
  3.1 0.8 %copy-start.4 = (s32[4]{0:T(128)S(1)}, s32[4]{0:T(128)}, u32[]{:S(2)}) copy-start(s32[4]{0:T(128)} %param.11) | copy-start | bytes 52
  3.1 0.7 %slice-start.1 = ((bf16[4,65,384]{2,0,1:T(4,128)(2,1)}), bf16[4,1,384]{2,0,1:T(4,128)(2,1)S(1)}, s32[]{:S(2)}) async-start(bf16[4,65,384]{2,0,1:T(4,128)(2,1)} %param.10), calls=%async_computation.1 | async-start | bytes 6144 | tf_op jit(solution)/shard_map/slice | solution.py:452
  3.1 0.9 %copy-start.2 = (bf16[3,2,4,4,65]{4,3,2,1,0:T(4,128)(2,1)S(1)}, bf16[3,2,4,4,65]{4,3,2,1,0:T(4,128)(2,1)}, u32[]{:S(2)}) copy-start(bf16[3,2,4,4,65]{4,3,2,1,0:T(4,128)(2,1)} %param.9) | copy-start | bytes 37444
  3.8 2.1 %copy-start = (bf16[2,256,64]{2,1,0:T(8,128)(2,1)S(1)}, bf16[2,256,64]{2,1,0:T(8,128)(2,1)}, u32[]{:S(2)}) copy-start(bf16[2,256,64]{2,1,0:T(8,128)(2,1)} %constant.23.clone.tab_t_ref) | copy-start | bytes 196612
  4.4 1.5 %copy-start.1 = (bf16[2,64,256]{2,1,0:T(8,128)(2,1)S(1)}, bf16[2,64,256]{2,1,0:T(8,128)(2,1)}, u32[]{:S(2)}) copy-start(bf16[2,64,256]{2,1,0:T(8,128)(2,1)} %constant.22.clone.tab_ref) | copy-start | bytes 196612
  5.1 0.8 %copy-start.5 = (f32[16]{0:T(128)S(1)}, f32[16]{0:T(128)}, u32[]{:S(2)}) copy-start(f32[16]{0:T(128)} %param.13) | copy-start | bytes 196

commit v3 on v2

--- a/solution.py
+++ b/solution.py
@@ -166,15 +166,16 @@
 
 
 def fused_kernel(
-    n_ma, n_row, pairs, rows, levels,
-    coef_ref, leg_ref, rest_ref, weight_ref, dif_ref, tab_ref, tab_t_ref,
+    n_ma, n_row, pairs, rows, levels, scale,
+    velocity_ref, vorticity_ref, legendre_ref, order_ref, weight_ref, dif_ref, tab_ref, tab_t_ref,
     out_ref,
-    coef_all, leg_all, rest_all, rest_t, onehot, spec, wgt, part, part_in, ext,
+    leg_ref, rest_ref, coef_all, leg_all, rest_all, rest_t, onehot, spec, wgt, part, part_in, ext,
     coef_send, coef_recv, leg_send, leg_recv, swap_send, swap_recv, rest_send, rest_recv, part_send, part_recv, halo_send, halo_recv,
 ):
     me = lax.axis_index("ma")
     row = lax.axis_index("row")
-    chunks, groups, wide_lanes = coef_ref.shape
+    _, chunks, groups, wide_lanes = coef_all.shape
+    coef_ref = coef_all.at[0]
     lanes = (chunks + 1) * wide_lanes
     fields2 = groups // 2
     orders = rows - 1
@@ -205,6 +206,39 @@
         )
     for side in (left, right):
         pl.semaphore_signal(barrier, inc=1, device_id=(me, side), device_id_type=pl.DeviceIdType.MESH)
+
+    per_chunk = pairs // chunks
+    packs = [
+        jnp.concatenate([velocity_ref[...].astype(f32)[:, p], vorticity_ref[...].astype(f32)[:, p]], axis=0)
+        for p in range(pairs)
+    ]
+    square = (wide_lanes, wide_lanes)
+    column = lax.broadcasted_iota(jnp.int32, (groups, wide_lanes), 1)
+    ends = jnp.zeros((groups, wide_lanes), f32)
+    for p in range(pairs):
+        ends = jnp.where(column == p, packs[p][:, orders:], ends)
+    ends = jnp.concatenate([ends, jnp.zeros((wide_lanes - groups, wide_lanes), f32)], axis=0)
+    ends = jnp.transpose(ends)[0:pairs, 0 : wide_lanes // 2]
+    tails = []
+    for c in range(chunks):
+        members = range(c * per_chunk, (c + 1) * per_chunk)
+        coef_all[0, c] = jnp.concatenate([packs[p][:, :orders] for p in members], axis=1).astype(bf16)
+        tables = [legendre_ref[p].astype(f32) for p in members]
+        turned = jnp.transpose(jnp.concatenate([t[:orders] for t in tables], axis=0)).astype(bf16)
+        for b in range(n_ma):
+            leg_ref[b, c] = turned[b * lat : (b + 1) * lat]
+        tails += [t[orders:] for t in tables]
+    tails = jnp.concatenate(tails, axis=0)
+    order_rows = [jnp.full((1, wide_lanes), order_ref[p].astype(f32)) for p in range(pairs)]
+    filler = jnp.zeros((pairs, wide_lanes // 2 - lat), f32)
+    for b in range(n_ma):
+        data_rows = jnp.concatenate([ends, tails[:, b * lat : (b + 1) * lat], filler], axis=1)
+        rest_ref[b] = jnp.concatenate([data_rows] + order_rows, axis=0).astype(bf16)
+    weight = jnp.zeros((1, lat), f32)
+    for b in range(n_ma):
+        weight = jnp.where(me == b, weight_ref[:, b * lat : (b + 1) * lat], weight)
+    weight = weight * scale
+
     pl.semaphore_wait(barrier, n_ma + 1)
 
     def coef_copy(s):
@@ -237,7 +271,6 @@
     coef_copy(1).start()
     leg_copy(1).start()
 
-    coef_all[0] = coef_ref[...]
     leg_all[0] = leg_ref[me]
     rest_all[0] = rest_ref[me]
 
@@ -289,7 +322,7 @@
             mask = even + odd if h == 0 else even - odd
             lhs = (coef[:, None, :] * mask[None]).reshape(groups * slots, lanes).astype(bf16)
             made = lax.dot_general(lhs, leg, (((1,), (1,)), ((), ())), preferred_element_type=f32)
-            spec[h, :, :, pl.ds(base, slots), :] = made.reshape(fields2, 2, slots, lat)
+            spec[h, :, pl.ds(base, slots), :] = made.reshape(groups, slots, lat)
         return carry
 
     for s in range(1, n_ma):
@@ -326,7 +359,6 @@
     to_spec = jnp.concatenate(
         [jnp.dot(hot, tab_ref[c], preferred_element_type=f32) for c in range(2)], axis=0
     ).astype(bf16)
-    weight = weight_ref[...]
 
     def middle(k, carry):
         halves = []
@@ -334,7 +366,8 @@
             grids = []
             for g in range(2):
                 for f in range(3):
-                    block = spec[h, g * 3 * levels + k * 3 + f].reshape(2 * full, lat).astype(bf16)
+                    at = (g * 3 + f) * 2 * levels + k
+                    block = jnp.concatenate([spec[h, at], spec[h, at + levels]], axis=0).astype(bf16)
                     grids.append(jnp.dot(to_grid, block, preferred_element_type=f32))
             u, w = grids[:3], grids[3:]
             lamb = [
@@ -347,8 +380,9 @@
             )
         for f in range(3):
             north, south = halves[0][f], halves[1][f]
-            wgt[0, k * 3 + f] = (weight * (north + south)).reshape(2, full, lat)
-            wgt[1, k * 3 + f] = (weight * (north - south)).reshape(2, full, lat)
+            for q, mixed in enumerate((weight * (north + south), weight * (north - south))):
+                for c in range(2):
+                    wgt[q, (f * 2 + c) * levels + k] = mixed[c * full : (c + 1) * full]
         return carry
 
     lax.fori_loop(0, levels, middle, 0)
@@ -360,7 +394,7 @@
         base = pl.multiple_of(d * slots, slots)
         total = None
         for q, mask in enumerate(masks(d)):
-            lhs = wgt[q, :, :, pl.ds(base, slots), :].reshape(fields2 * slots, lat).astype(bf16)
+            lhs = wgt[q, :, pl.ds(base, slots), :].reshape(fields2 * slots, lat).astype(bf16)
             made = jnp.dot(lhs, leg_of(d), preferred_element_type=f32)
             made = made.reshape(fields2, slots, lanes) * mask[None]
             total = made if total is None else total + made
@@ -387,8 +421,9 @@
     own_tail = rest_t[0:fields2, :]
     heads = [source[:, c * wide_lanes : (c + 1) * wide_lanes] + coef_ref[c, 0:fields2].astype(f32) for c in range(chunks)]
     source = jnp.concatenate(heads + [tail + own_tail], axis=1)
-    source = source.reshape(levels, fields2 // levels, lanes)
-    ext[2 : levels + 2] = source
+    source = source.reshape(fields2 // levels, levels, lanes)
+    for k in range(levels):
+        ext[k + 2] = source[:, k, :]
     to_left = remote(ext.at[2:4], ext.at[levels + 2 : levels + 4], halo_send.at[0], halo_recv.at[0], (me, left))
     to_right = remote(ext.at[levels : levels + 2], ext.at[0:2], halo_send.at[1], halo_recv.at[1], (me, right))
     to_left.start()
@@ -410,7 +445,7 @@
     for i in range(2):
         wide[i] = wide[i] * has_left
         wide[levels + 2 + i] = wide[levels + 2 + i] * has_right
-    coupling = [jnp.full(shape, dif_ref[row * levels + i]) for i in range(levels + 4)]
+    coupling = [jnp.full(shape, dif_ref[lax.rem((row + n_row) * levels + i - 2, n_row * levels)]) for i in range(levels + 4)]
     inverse = [1.0 / (1.0 + 2.0 * c) for c in coupling]
     first = [
         (wide[i] + coupling[i] * (wide[i - 1] + wide[i + 1])) * inverse[i] for i in range(1, levels + 3)
@@ -439,41 +474,28 @@
     bf16 = jnp.bfloat16
     f32 = jnp.float32
     groups = 12 * levels
-    heads, tails = [], []
-    for x in (velocity, vorticity):
-        x = jnp.transpose(x, (2, 0, 1, 3, 4))
-        heads.append(x[..., :orders].reshape(6 * levels, chunks, 128))
-        tails.append(x[..., orders].reshape(6 * levels, pairs))
-    coef = jnp.transpose(jnp.concatenate(heads, axis=0), (1, 0, 2))
-    leg = legendre[:, :orders].reshape(chunks, 128, n_ma, lat)
-    leg = jnp.transpose(leg, (2, 0, 3, 1))
-    coef_tail = jnp.transpose(jnp.concatenate(tails, axis=0))
-    coef_tail = jnp.pad(coef_tail, ((0, 0), (0, 64 - groups)))
-    leg_tail = jnp.transpose(legendre[:, orders].reshape(pairs, n_ma, lat), (1, 0, 2))
-    leg_tail = jnp.pad(leg_tail, ((0, 0), (0, 0), (0, 64 - lat)))
-    tail = jnp.concatenate([jnp.broadcast_to(coef_tail, (n_ma, pairs, 64)), leg_tail], axis=2)
-    order_rows = jnp.broadcast_to(pair_order.astype(bf16)[None, :, None], (n_ma, pairs, 128))
-    rest = jnp.concatenate([tail, order_rows], axis=1)
     scale = (NLON / points) / math.sqrt(NLON) / orders
-    weight = lax.dynamic_slice_in_dim(lat_weight, lax.axis_index("ma") * lat, lat) * scale
     angle = np.outer(np.arange(orders), np.arange(points)) % points * (2.0 * math.pi / points)
     table = np.stack([np.cos(angle), -np.sin(angle)])
     tab = jnp.asarray(table, bf16)
     tab_t = jnp.asarray(np.transpose(table, (0, 2, 1)), bf16)
     vmem = pl.BlockSpec(memory_space=pltpu.VMEM)
+    smem = pl.BlockSpec(memory_space=pltpu.SMEM)
     out = pl.pallas_call(
-        functools.partial(fused_kernel, n_ma, n_row, pairs, rows, levels),
+        functools.partial(fused_kernel, n_ma, n_row, pairs, rows, levels, scale),
         out_shape=jax.ShapeDtypeStruct((levels, 6, used), f32),
-        in_specs=[vmem, vmem, vmem, vmem, pl.BlockSpec(memory_space=pltpu.SMEM), vmem, vmem],
+        in_specs=[vmem, vmem, vmem, smem, vmem, smem, vmem, vmem],
         out_specs=vmem,
         scratch_shapes=[
+            pltpu.VMEM((n_ma, chunks, lat, 128), bf16),
+            pltpu.VMEM((n_ma, 8, 128), bf16),
             pltpu.VMEM((n_ma, chunks, groups, 128), bf16),
             pltpu.VMEM((n_ma, chunks, lat, 128), bf16),
             pltpu.VMEM((n_ma, 8, 128), bf16),
             pltpu.VMEM((128, 128), f32),
             pltpu.VMEM((full, orders), f32),
-            pltpu.VMEM((2, groups // 2, 2, full, lat), f32),
-            pltpu.VMEM((2, 3 * levels, 2, full, lat), f32),
+            pltpu.VMEM((2, groups, full, lat), f32),
+            pltpu.VMEM((2, groups // 2, full, lat), f32),
             pltpu.VMEM((n_ma, groups // 2, lanes), bf16),
             pltpu.VMEM((n_ma, groups // 2, lanes), bf16),
             pltpu.VMEM((levels + 4, 6, lanes), f32),
@@ -483,7 +505,16 @@
         compiler_params=pltpu.CompilerParams(
             collective_id=0, has_side_effects=True, vmem_limit_bytes=48 * 1024 * 1024
         ),
-    )(coef, leg, rest, weight[None], jnp.pad(diffusivity, (2, 2)), tab, tab_t)
+    )(
+        velocity.reshape(6 * levels, pairs, rows),
+        vorticity.reshape(6 * levels, pairs, rows),
+        legendre,
+        pair_order,
+        lat_weight[None],
+        diffusivity,
+        tab,
+        tab_t,
+    )
     out = jnp.concatenate(
         [out[..., :main].reshape(levels, 6, pairs, orders), out[..., main:, None]], axis=3
     )

time: 35.3 us -> 31.9 us (0.904)
  local copies, waits for them, and re-layouts: 5.23 us -> 2.12 us
  other arithmetic: 1.67 us -> 0.72 us
  Pallas kernels: 27.9 us -> 28.8 us
    slice x11 -> x0, local copies, waits for them, and re-layouts: 3.33 us -> none  [the longest x3 1.21 us: fused(): leg = legendre[:, :orders].reshape(chunks, 128, n_ma, lat)]
    unnamed x12 -> x15, local copies, waits for them, and re-layouts: 0.66 us -> 1.74 us
    pallas_call x1, Pallas kernels: 27.9 us -> 28.8 us  [fused(): pl.pallas_call(functools.partial(fused_kernel, n_ma, n_row, pairs, rows,...]
    broadcast_in_dim x1 -> x0, other arithmetic: 0.76 us -> none  [fused(): weight[None]]
    reshape x6 -> x0, local copies, waits for them, and re-layouts: 0.42 us -> none  [the longest x2 0.23 us: fused(): leg = legendre[:, :orders].reshape(chunks, 128, n_ma, lat)]
where the time goes in v3:
time: 31.9 us; the launch traced here: 31.7 us
  Pallas kernels  28.8 us (90%)
  local copies, waits for them, and re-layouts  2.12 us (7%)
  other arithmetic  0.72 us (2%)
    pallas_call x1, Pallas kernels, fused(): pl.pallas_call(functools.partial(fused_kernel, n_ma, n_row, pairs, rows,...  28.8 us
    unnamed x15, local copies, waits for them, and re-layouts  1.74 us
    transpose x1, other arithmetic, fused(): jnp.transpose(out.reshape(levels, 3, 2, pairs, rows), (1, 2, 0, 3, 4))  0.72 us

profile of v3, /device:TPU:1, one launch (start us, length us, event | category | flops | bytes accessed | tf_op | source)
XLA Modules:
  0.0 31.7 jit_solution(12640354595935567153)
XLA Ops:
  0.0 0.0 copy-start.6
  0.0 0.7 %copy-done.6 = f32[384]{0:T(512)S(1)} copy-done((f32[384]{0:T(512)S(1)}, f32[384]{0:T(512)}, u32[]{:S(2)}) %copy-start.6) | copy-done | bytes 1560
  0.7 0.0 copy-start
  0.7 0.0 copy-start.1
  0.7 0.0 copy-start.2
  0.7 0.0 copy-start.3
  0.7 0.0 copy-start.4
  0.7 0.0 copy-start.5
  0.7 1.0 %copy.13.legendre_ref = bf16[4,65,384]{2,1,0:T(8,128)(2,1)S(1)} copy(bf16[4,65,384]{2,0,1:T(4,128)(2,1)} %param.10) | data formatting | bytes 399360 | tf_op args[2]
  1.8 0.0 copy-done
  1.8 0.0 copy-done.1
  1.8 0.0 copy-done.2
  1.8 0.0 copy-done.3
  1.8 0.0 copy-done.4
  1.8 0.0 copy-done.5
  1.8 28.8 %shard_map.82 = f32[4,6,260]{2,1,0:T(8,128)S(1)} custom-call(bf16[24,4,65]{2,1,0:T(4,128)(2,1)S(1)} %bitcast.7, bf16[24,4,65]{2,1,0:T(4,128)(2,1)S(1)} %bitcast.8, bf16[4,65,384]{2,1,0:T(8,128)(2,1)S(1)} %copy.13.legendre_ref, s32[4]{0:T(128)S(1)} %copy-done.4, f32[1,384]{1,0:T(1,128)S(1)} %broadcast_in_dim.4.weight_ref, f32[16]{0:T(128)S(1)} %copy-done.5, ...), custom_call_target="tpu_custom_call" | custom-call | tf_op jit(solution)/shard_map/pallas_call | solution.py:484
  30.6 0.1 concatenate.8
  30.7 0.3 copy.16
  31.0 0.7 %maximum_bitcast_fusion = f32[3,2,4,4,65]{4,3,2,1,0:T(4,128)} fusion(f32[4,3,2,4,1]{4,3,0,2,1:T(4,128)S(1)} %copy.16, f32[4,3,2,4,64]{4,3,0,2,1:T(4,128)S(1)} %concatenate.8), kind=kLoop, calls=%fused_computation | loop fusion | flops 6240 | bytes 49920 | tf_op jit(solution)/shard_map/transpose | solution.py:521
  (5 shorter events, 0.0 us)
Async XLA Ops:
  0.0 0.7 %copy-start.6 = (f32[384]{0:T(512)S(1)}, f32[384]{0:T(512)}, u32[]{:S(2)}) copy-start(f32[384]{0:T(512)} %param.12) | copy-start | bytes 4612
  0.7 1.1 %copy-start = (bf16[2,256,64]{2,1,0:T(8,128)(2,1)S(1)}, bf16[2,256,64]{2,1,0:T(8,128)(2,1)}, u32[]{:S(2)}) copy-start(bf16[2,256,64]{2,1,0:T(8,128)(2,1)} %constant.5.clone.tab_t_ref) | copy-start | bytes 196612
  0.7 1.1 %copy-start.1 = (bf16[2,64,256]{2,1,0:T(8,128)(2,1)S(1)}, bf16[2,64,256]{2,1,0:T(8,128)(2,1)}, u32[]{:S(2)}) copy-start(bf16[2,64,256]{2,1,0:T(8,128)(2,1)} %constant.4.clone.tab_ref) | copy-start | bytes 196612
  0.7 1.1 %copy-start.2 = (bf16[3,2,4,4,65]{4,3,2,1,0:T(4,128)(2,1)S(1)}, bf16[3,2,4,4,65]{4,3,2,1,0:T(4,128)(2,1)}, u32[]{:S(2)}) copy-start(bf16[3,2,4,4,65]{4,3,2,1,0:T(4,128)(2,1)} %param.8) | copy-start | bytes 37444
  0.7 1.1 %copy-start.3 = (bf16[3,2,4,4,65]{4,3,2,1,0:T(4,128)(2,1)S(1)}, bf16[3,2,4,4,65]{4,3,2,1,0:T(4,128)(2,1)}, u32[]{:S(2)}) copy-start(bf16[3,2,4,4,65]{4,3,2,1,0:T(4,128)(2,1)} %param.9) | copy-start | bytes 37444
  0.7 1.1 %copy-start.4 = (s32[4]{0:T(128)S(1)}, s32[4]{0:T(128)}, u32[]{:S(2)}) copy-start(s32[4]{0:T(128)} %order_ref.1) | copy-start | bytes 52
  0.7 1.1 %copy-start.5 = (f32[16]{0:T(128)S(1)}, f32[16]{0:T(128)}, u32[]{:S(2)}) copy-start(f32[16]{0:T(128)} %dif_ref.1) | copy-start | bytes 196

commit v4 on v3

--- a/solution.py
+++ b/solution.py
@@ -169,7 +169,7 @@
     n_ma, n_row, pairs, rows, levels, scale,
     velocity_ref, vorticity_ref, legendre_ref, order_ref, weight_ref, dif_ref, tab_ref, tab_t_ref,
     out_ref,
-    leg_ref, rest_ref, coef_all, leg_all, rest_all, rest_t, onehot, spec, wgt, part, part_in, ext,
+    leg_ref, rest_ref, coef_all, leg_all, rest_all, rest_t, spec, wgt, part, part_in, ext,
     coef_send, coef_recv, leg_send, leg_recv, swap_send, swap_recv, rest_send, rest_recv, part_send, part_recv, halo_send, halo_recv,
 ):
     me = lax.axis_index("ma")
@@ -220,10 +220,11 @@
     ends = jnp.concatenate([ends, jnp.zeros((wide_lanes - groups, wide_lanes), f32)], axis=0)
     ends = jnp.transpose(ends)[0:pairs, 0 : wide_lanes // 2]
     tails = []
+    all_tables = legendre_ref[...].astype(f32)
     for c in range(chunks):
         members = range(c * per_chunk, (c + 1) * per_chunk)
         coef_all[0, c] = jnp.concatenate([packs[p][:, :orders] for p in members], axis=1).astype(bf16)
-        tables = [legendre_ref[p].astype(f32) for p in members]
+        tables = [all_tables[:, p] for p in members]
         turned = jnp.transpose(jnp.concatenate([t[:orders] for t in tables], axis=0)).astype(bf16)
         for b in range(n_ma):
             leg_ref[b, c] = turned[b * lat : (b + 1) * lat]
@@ -235,9 +236,10 @@
         data_rows = jnp.concatenate([ends, tails[:, b * lat : (b + 1) * lat], filler], axis=1)
         rest_ref[b] = jnp.concatenate([data_rows] + order_rows, axis=0).astype(bf16)
     weight = jnp.zeros((1, lat), f32)
+    all_weights = weight_ref[...].reshape(1, n_ma * lat)
     for b in range(n_ma):
-        weight = jnp.where(me == b, weight_ref[:, b * lat : (b + 1) * lat], weight)
-    weight = weight * scale
+        weight = jnp.where(me == b, all_weights[:, b * lat : (b + 1) * lat], weight)
+    weight = jnp.concatenate([weight, weight], axis=1) * scale
 
     pl.semaphore_wait(barrier, n_ma + 1)
 
@@ -305,25 +307,50 @@
         tail = rest_t[wide_lanes // 2 : wide_lanes // 2 + lat, :].astype(bf16)
         return jnp.concatenate([leg_all[d, c] for c in range(chunks)] + [tail], axis=1)
 
-    def synth(d, carry):
+    def place(d):
         values = lows(d)
         order = jnp.zeros((slots, orders), jnp.int32)
         for p in range(pairs):
             order = jnp.where(m_sub == 2 * p, values[p], order)
             order = jnp.where(m_sub == 2 * p + 1, orders - 1 - values[p], order)
-        base = pl.multiple_of(d * slots, slots)
-        onehot[pl.ds(base, slots), :] = (m_lane == order).astype(f32)
+        return (m_lane == order).astype(f32)
+
+    def both(leg):
+        return jnp.concatenate([leg, leg], axis=0), jnp.concatenate([leg, -leg], axis=0)
+
+    def synth(d):
         even, odd = masks(d)
         coef = jnp.concatenate(
             [coef_all[d, c].astype(f32) for c in range(chunks)] + [rest_t[0:groups, :]], axis=1
         )
         leg = leg_of(d)
-        for h in range(2):
-            mask = even + odd if h == 0 else even - odd
-            lhs = (coef[:, None, :] * mask[None]).reshape(groups * slots, lanes).astype(bf16)
-            made = lax.dot_general(lhs, leg, (((1,), (1,)), ((), ())), preferred_element_type=f32)
-            spec[h, :, pl.ds(base, slots), :] = made.reshape(groups, slots, lat)
-        return carry
+        lhs = [
+            (coef[:, None, :] * mask[None]).reshape(groups * slots, lanes).astype(bf16)
+            for mask in (even, odd)
+        ]
+        made = lax.dot_general(
+            jnp.concatenate(lhs, axis=1),
+            jnp.concatenate(both(leg), axis=1),
+            (((1,), (1,)), ((), ())),
+            preferred_element_type=f32,
+        )
+        spec[:, d * slots : (d + 1) * slots, :] = made.reshape(groups, slots, 2 * lat)
+
+    full = n_ma * slots
+
+    def grid_tables():
+        hot = jnp.concatenate([place(d) for d in range(n_ma)], axis=0).astype(bf16)
+        to_grid = jnp.concatenate(
+            [
+                lax.dot_general(tab_t_ref[c], hot, (((1,), (1,)), ((), ())), preferred_element_type=f32)
+                for c in range(2)
+            ],
+            axis=1,
+        ).astype(bf16)
+        to_spec = jnp.concatenate(
+            [jnp.dot(hot, tab_ref[c], preferred_element_type=f32) for c in range(2)], axis=0
+        ).astype(bf16)
+        return to_grid, to_spec
 
     for s in range(1, n_ma):
         rest_copy(s).wait_recv()
@@ -338,51 +365,36 @@
         for t in (s, s + 1):
             leg_copy(t).wait_recv()
             swap_copy(t).start()
-    synth(0, 0)
+        if s == 2:
+            to_grid, to_spec = grid_tables()
+        if s == n_ma - 4:
+            synth(0)
+    if n_ma < 6:
+        synth(0)
     for s in range(1, n_ma):
         if s % 2 == 1:
             coef_copy(s).wait_recv()
         remote(
             leg_all.at[s, half], leg_all.at[s, 1 - half], swap_send.at[s], swap_recv.at[s], (me, mate_row)
         ).wait_recv()
-        synth(s, 0)
-
-    hot = onehot[...].astype(bf16)
-    full = n_ma * slots
-    to_grid = jnp.concatenate(
-        [
-            lax.dot_general(tab_t_ref[c], hot, (((1,), (1,)), ((), ())), preferred_element_type=f32)
-            for c in range(2)
-        ],
-        axis=1,
-    ).astype(bf16)
-    to_spec = jnp.concatenate(
-        [jnp.dot(hot, tab_ref[c], preferred_element_type=f32) for c in range(2)], axis=0
-    ).astype(bf16)
+        synth(s)
 
     def middle(k, carry):
-        halves = []
-        for h in range(2):
-            grids = []
-            for g in range(2):
-                for f in range(3):
-                    at = (g * 3 + f) * 2 * levels + k
-                    block = jnp.concatenate([spec[h, at], spec[h, at + levels]], axis=0).astype(bf16)
-                    grids.append(jnp.dot(to_grid, block, preferred_element_type=f32))
-            u, w = grids[:3], grids[3:]
-            lamb = [
-                u[1] * w[2] - u[2] * w[1],
-                u[2] * w[0] - u[0] * w[2],
-                u[0] * w[1] - u[1] * w[0],
-            ]
-            halves.append(
-                [jnp.dot(to_spec, x.astype(bf16), preferred_element_type=f32) for x in lamb]
-            )
+        grids = []
+        for gf in range(6):
+            at = gf * 2 * levels + k
+            block = jnp.concatenate([spec[at], spec[at + levels]], axis=0).astype(bf16)
+            grids.append(jnp.dot(to_grid, block, preferred_element_type=f32))
+        u, w = grids[:3], grids[3:]
+        lamb = [
+            u[1] * w[2] - u[2] * w[1],
+            u[2] * w[0] - u[0] * w[2],
+            u[0] * w[1] - u[1] * w[0],
+        ]
         for f in range(3):
-            north, south = halves[0][f], halves[1][f]
-            for q, mixed in enumerate((weight * (north + south), weight * (north - south))):
-                for c in range(2):
-                    wgt[q, (f * 2 + c) * levels + k] = mixed[c * full : (c + 1) * full]
+            made = weight * jnp.dot(to_spec, lamb[f].astype(bf16), preferred_element_type=f32)
+            for c in range(2):
+                wgt[(f * 2 + c) * levels + k] = made[c * full : (c + 1) * full]
         return carry
 
     lax.fori_loop(0, levels, middle, 0)
@@ -393,9 +405,9 @@
     def analyse(d):
         base = pl.multiple_of(d * slots, slots)
         total = None
-        for q, mask in enumerate(masks(d)):
-            lhs = wgt[q, :, pl.ds(base, slots), :].reshape(fields2 * slots, lat).astype(bf16)
-            made = jnp.dot(lhs, leg_of(d), preferred_element_type=f32)
+        lhs = wgt[:, pl.ds(base, slots), :].reshape(fields2 * slots, 2 * lat).astype(bf16)
+        for leg, mask in zip(both(leg_of(d)), masks(d)):
+            made = jnp.dot(lhs, leg, preferred_element_type=f32)
             made = made.reshape(fields2, slots, lanes) * mask[None]
             total = made if total is None else total + made
         return jnp.sum(total, axis=1)
@@ -493,9 +505,8 @@
             pltpu.VMEM((n_ma, chunks, lat, 128), bf16),
             pltpu.VMEM((n_ma, 8, 128), bf16),
             pltpu.VMEM((128, 128), f32),
-            pltpu.VMEM((full, orders), f32),
-            pltpu.VMEM((2, groups, full, lat), f32),
-            pltpu.VMEM((2, groups // 2, full, lat), f32),
+            pltpu.VMEM((groups, full, 2 * lat), f32),
+            pltpu.VMEM((groups // 2, full, 2 * lat), f32),
             pltpu.VMEM((n_ma, groups // 2, lanes), bf16),
             pltpu.VMEM((n_ma, groups // 2, lanes), bf16),
             pltpu.VMEM((levels + 4, 6, lanes), f32),
@@ -508,9 +519,9 @@
     )(
         velocity.reshape(6 * levels, pairs, rows),
         vorticity.reshape(6 * levels, pairs, rows),
-        legendre,
+        jnp.transpose(legendre, (1, 0, 2)),
         pair_order,
-        lat_weight[None],
+        lat_weight,
         diffusivity,
         tab,
         tab_t,

time: 31.9 us -> 33.7 us (1.056)
  local copies, waits for them, and re-layouts: 2.12 us -> 5.2 us
  Pallas kernels: 28.8 us -> 27.4 us
    unnamed x15 -> x16, local copies, waits for them, and re-layouts: 1.74 us -> 4.83 us
    pallas_call x1, Pallas kernels: 28.8 us -> 27.4 us  [fused(): pl.pallas_call(functools.partial(fused_kernel, n_ma, n_row, pairs, rows,...]
where the time goes in v4:
time: 33.7 us; the launch traced here: 33.4 us
  Pallas kernels  27.4 us (81%)
  local copies, waits for them, and re-layouts  5.2 us (15%)
  other arithmetic  0.72 us (2%)
    pallas_call x1, Pallas kernels, fused(): pl.pallas_call(functools.partial(fused_kernel, n_ma, n_row, pairs, rows,...  27.4 us
    unnamed x16, local copies, waits for them, and re-layouts  4.83 us
    transpose x1, other arithmetic, fused(): jnp.transpose(out.reshape(levels, 3, 2, pairs, rows), (1, 2, 0, 3, 4))  0.72 us

profile of v4, /device:TPU:1, one launch (start us, length us, event | category | flops | bytes accessed | tf_op | source)
XLA Modules:
  0.0 33.4 jit_solution(8247245680905433850)
XLA Ops:
  0.0 0.0 copy-start.5
  0.0 0.0 copy-start.6
  0.0 0.0 copy-start.7
  0.0 0.7 %copy-done.5 = f32[384]{0:T(512)S(1)} copy-done((f32[384]{0:T(512)S(1)}, f32[384]{0:T(512)}, u32[]{:S(2)}) %copy-start.5) | copy-done | bytes 1560
  0.7 0.0 copy-done.6
  0.7 0.0 copy-done.7
  0.7 0.0 copy-start
  0.7 0.9 %copy-done = bf16[4,65,384]{2,0,1:T(4,128)(2,1)S(1)} copy-done((bf16[4,65,384]{2,0,1:T(4,128)(2,1)S(1)}, bf16[4,65,384]{2,0,1:T(4,128)(2,1)}, u32[]{:S(2)}) %copy-start) | copy-done | bytes 199704
  1.6 0.0 copy-start.1
  1.6 0.9 %copy-done.1 = bf16[2,256,64]{2,1,0:T(8,128)(2,1)S(1)} copy-done((bf16[2,256,64]{2,1,0:T(8,128)(2,1)S(1)}, bf16[2,256,64]{2,1,0:T(8,128)(2,1)}, u32[]{:S(2)}) %copy-start.1) | copy-done | bytes 65560
  2.5 0.0 copy-start.2
  2.5 0.8 %copy-done.2 = bf16[2,64,256]{2,1,0:T(8,128)(2,1)S(1)} copy-done((bf16[2,64,256]{2,1,0:T(8,128)(2,1)S(1)}, bf16[2,64,256]{2,1,0:T(8,128)(2,1)}, u32[]{:S(2)}) %copy-start.2) | copy-done | bytes 65560
  3.4 0.0 copy-start.3
  3.4 0.7 %copy-done.3 = bf16[3,2,4,4,65]{4,3,2,1,0:T(4,128)(2,1)S(1)} copy-done((bf16[3,2,4,4,65]{4,3,2,1,0:T(4,128)(2,1)S(1)}, bf16[3,2,4,4,65]{4,3,2,1,0:T(4,128)(2,1)}, u32[]{:S(2)}) %copy-start.3) | copy-done | bytes 12504
  4.1 0.0 copy-start.4
  4.1 0.7 %copy-done.4 = bf16[3,2,4,4,65]{4,3,2,1,0:T(4,128)(2,1)S(1)} copy-done((bf16[3,2,4,4,65]{4,3,2,1,0:T(4,128)(2,1)S(1)}, bf16[3,2,4,4,65]{4,3,2,1,0:T(4,128)(2,1)}, u32[]{:S(2)}) %copy-start.4) | copy-done | bytes 12504
  4.8 27.4 %shard_map.82 = f32[4,6,260]{2,1,0:T(8,128)S(1)} custom-call(bf16[24,4,65]{2,1,0:T(4,128)(2,1)S(1)} %bitcast.9, bf16[24,4,65]{2,1,0:T(4,128)(2,1)S(1)} %bitcast.10, bf16[65,4,384]{2,1,0:T(4,128)(2,1)S(1)} %bitcast.8, s32[4]{0:T(128)S(1)} %copy-done.6, f32[384]{0:T(512)S(1)} %copy-done.5, f32[16]{0:T(128)S(1)} %copy-done.7, ...), custom_call_target="tpu_custom_call" | custom-call | tf_op jit(solution)/shard_map/pallas_call | solution.py:496
  32.3 0.1 concatenate.8
  32.4 0.3 copy.14
  32.7 0.7 %maximum_bitcast_fusion = f32[3,2,4,4,65]{4,3,2,1,0:T(4,128)} fusion(f32[4,3,2,4,1]{4,3,0,2,1:T(4,128)S(1)} %copy.14, f32[4,3,2,4,64]{4,3,0,2,1:T(4,128)S(1)} %concatenate.8), kind=kLoop, calls=%fused_computation | loop fusion | flops 6240 | bytes 49920 | tf_op jit(solution)/shard_map/transpose | solution.py:532
  (4 shorter events, 0.0 us)
Async XLA Ops:
  0.0 0.7 %copy-start.5 = (f32[384]{0:T(512)S(1)}, f32[384]{0:T(512)}, u32[]{:S(2)}) copy-start(f32[384]{0:T(512)} %weight_ref.1) | copy-start | bytes 4612
  0.0 0.7 %copy-start.6 = (s32[4]{0:T(128)S(1)}, s32[4]{0:T(128)}, u32[]{:S(2)}) copy-start(s32[4]{0:T(128)} %order_ref.1) | copy-start | bytes 52
  0.0 0.7 %copy-start.7 = (f32[16]{0:T(128)S(1)}, f32[16]{0:T(128)}, u32[]{:S(2)}) copy-start(f32[16]{0:T(128)} %dif_ref.1) | copy-start | bytes 196
  0.7 0.9 %copy-start = (bf16[4,65,384]{2,0,1:T(4,128)(2,1)S(1)}, bf16[4,65,384]{2,0,1:T(4,128)(2,1)}, u32[]{:S(2)}) copy-start(bf16[4,65,384]{2,0,1:T(4,128)(2,1)} %param.10) | copy-start | bytes 599044
  1.6 0.9 %copy-start.1 = (bf16[2,256,64]{2,1,0:T(8,128)(2,1)S(1)}, bf16[2,256,64]{2,1,0:T(8,128)(2,1)}, u32[]{:S(2)}) copy-start(bf16[2,256,64]{2,1,0:T(8,128)(2,1)} %constant.5.clone.tab_t_ref) | copy-start | bytes 196612
  2.5 0.8 %copy-start.2 = (bf16[2,64,256]{2,1,0:T(8,128)(2,1)S(1)}, bf16[2,64,256]{2,1,0:T(8,128)(2,1)}, u32[]{:S(2)}) copy-start(bf16[2,64,256]{2,1,0:T(8,128)(2,1)} %constant.4.clone.tab_ref) | copy-start | bytes 196612
  3.4 0.7 %copy-start.3 = (bf16[3,2,4,4,65]{4,3,2,1,0:T(4,128)(2,1)S(1)}, bf16[3,2,4,4,65]{4,3,2,1,0:T(4,128)(2,1)}, u32[]{:S(2)}) copy-start(bf16[3,2,4,4,65]{4,3,2,1,0:T(4,128)(2,1)} %param.8) | copy-start | bytes 37444
  4.1 0.7 %copy-start.4 = (bf16[3,2,4,4,65]{4,3,2,1,0:T(4,128)(2,1)S(1)}, bf16[3,2,4,4,65]{4,3,2,1,0:T(4,128)(2,1)}, u32[]{:S(2)}) copy-start(bf16[3,2,4,4,65]{4,3,2,1,0:T(4,128)(2,1)} %param.9) | copy-start | bytes 37444
